TPU v7x, 32 devices: a whole 2x2x4 slice. The times are simulated.
32 devices in a mesh: row: 4 (over y, x), col: 8 (over z, core).
Axes of the slice: x: 2, y: 2, z: 4, core: 2. Of those that a mesh axis runs over, the one named last changes fastest.
Arguments:
- node_features: bfloat16 [4096, 1024], P(('row', 'col')), may hold values from -6 to 6
- norm_gain: float32 [1024], replicated, may hold values from 0.5 to 1.5
- w_query: bfloat16 [1024, 1024], replicated, may hold values from -0.1875 to 0.1875
- w_keyvalue: bfloat16 [1024, 2048], replicated, may hold values from -0.1875 to 0.1875
- w_out: bfloat16 [1024, 1024], replicated, may hold values from -0.1875 to 0.1875
- bias_table: float32 [32, 8], replicated, may hold values from -4 to 4
- edge_slope: float32 [8], replicated, may hold values from 0.5 to 1.5
- pair_blocks: int32 [4, 8, 2, 16], P('row', 'col'), may hold values from -1 to 7, as said below
- bucket_ids: int32 [4, 8, 16, 128, 128], P('row', 'col'), may hold values from 0 to 31
- edge_weight: bfloat16 [4, 8, 4, 4, 128, 128], P('row', 'col'), may hold values from -4 to 240
Outputs:
- node_out: bfloat16 [4096, 1024], P(('row', 'col'))
Inputs may be any that keep to these rules, and one draw needn't show every extreme that they name: `pair_blocks`: slots of a tile with query block -1 are empty and name key block 0. The listed pairs of a tile are distinct; each tile (r, c) lists, among the slots from t = r, every block of node shard r * 8 + c paired with itself. Up to 4 slots from one owner to one row range are used, and some tile uses all 16 of its slots.
All inputs are finite; a program needn't handle non-finite values.
Results may differ from a plain program's by a relative error of at most 0.005.
Values may be sent and summed in bfloat16 or wider, within the bound.
A program may use at most 256 MiB of HBM per device.

v0:
```python
import math

import jax
import jax.numpy as jnp
from jax import lax
from jax.sharding import PartitionSpec as P

EPSILON = 1e-05
LOW_FLOOR = -1e30


def normalize(features, gain_vec):
    as_float = features.astype(jnp.float32)
    centered = as_float - jnp.mean(as_float, axis=-1, keepdims=True)
    variance = jnp.mean(centered * centered, axis=-1, keepdims=True)
    return (centered * lax.rsqrt(variance + EPSILON) * gain_vec).astype(jnp.bfloat16)


def local(
    node_features,
    norm_gain,
    w_query,
    w_keyvalue,
    w_out,
    bias_table,
    edge_slope,
    pair_blocks,
    bucket_ids,
    edge_weight,
):
    rows_own, model_width = node_features.shape
    head_count = edge_slope.shape[0]
    head_dim = model_width // head_count
    tile_size = bucket_ids.shape[-1]
    bucket_count = bias_table.shape[0]
    normalized = normalize(node_features, norm_gain)
    queries = jnp.dot(normalized, w_query, preferred_element_type=jnp.float32).astype(jnp.bfloat16)
    query_range = lax.all_gather(queries, "col", axis=0, tiled=True)
    key_value = jnp.dot(normalized, w_keyvalue, preferred_element_type=jnp.float32).astype(
        jnp.bfloat16
    )
    key_group = lax.all_gather(key_value, "row", axis=0, tiled=True)
    arrived = lax.all_to_all(edge_weight, "row", split_axis=2, concat_axis=0, tiled=True)
    slot_count = arrived.shape[0] * arrived.shape[3]
    edge_values = arrived.reshape(slot_count, tile_size, tile_size)
    pair_table = pair_blocks.reshape(2, slot_count)
    bucket_tiles = bucket_ids.reshape(slot_count, tile_size, tile_size)
    query_count = query_range.shape[0] // tile_size
    slot_cap = slot_count // lax.axis_size("row")
    key_blocks = rows_own // tile_size
    query_block = pair_table[0]
    key_block = pair_table[1] + jnp.arange(slot_count, dtype=jnp.int32) // slot_cap * key_blocks
    query_flat = query_range.reshape(query_count, tile_size * model_width)
    key_count = key_group.shape[0] // tile_size
    key_flat = key_group.reshape(key_count, tile_size * 2 * model_width)
    query_ids = jnp.arange(query_count, dtype=jnp.int32)
    key_ids = jnp.arange(key_count, dtype=jnp.int32)
    bucket_range = jnp.arange(bucket_count, dtype=jnp.int32)
    batch_size = math.gcd(slot_count, max(1, 512 // tile_size))
    turn_count = slot_count // batch_size
    score_scale = head_dim ** (-0.5)

    def score_slots(inputs):
        query_index, key_index, tile_weights, tile_buckets = inputs
        query_pick = (jnp.maximum(query_index, 0)[:, None] == query_ids[None, :]).astype(
            jnp.bfloat16
        )
        key_pick = (key_index[:, None] == key_ids[None, :]).astype(jnp.bfloat16)
        query_sel = jnp.dot(query_pick, query_flat, preferred_element_type=jnp.float32).astype(
            jnp.bfloat16
        )
        query_sel = query_sel.reshape(batch_size, tile_size, head_count, head_dim)
        pair_sel = jnp.dot(key_pick, key_flat, preferred_element_type=jnp.float32).astype(
            jnp.bfloat16
        )
        pair_sel = pair_sel.reshape(batch_size, tile_size, 2, head_count, head_dim)
        key_sel = pair_sel[:, :, 0]
        value_sel = pair_sel[:, :, 1]
        raw_score = (
            jnp.einsum("sihd,sjhd->shij", query_sel, key_sel, preferred_element_type=jnp.float32)
            * score_scale
        )
        bucket_hot = (tile_buckets[..., None] == bucket_range).astype(jnp.float32)
        lookup = jnp.einsum(
            "sijb,bh->shij", bucket_hot, bias_table, precision=lax.Precision.HIGHEST
        )
        raw_score = (
            raw_score
            + lookup
            + edge_slope[None, :, None, None] * tile_weights.astype(jnp.float32)[:, None]
        )
        row_max = jnp.max(raw_score, axis=-1)
        prob_vals = jnp.exp(raw_score - row_max[..., None]).astype(jnp.bfloat16)
        row_sum = jnp.sum(prob_vals.astype(jnp.float32), axis=-1)
        weighted = jnp.einsum(
            "shij,sjhd->sihd", prob_vals, value_sel, preferred_element_type=jnp.float32
        )
        return (row_max, row_sum, weighted)

    row_max, row_sum, weighted = lax.map(
        score_slots,
        (
            query_block.reshape(turn_count, batch_size),
            key_block.reshape(turn_count, batch_size),
            edge_values.reshape(turn_count, batch_size, tile_size, tile_size),
            bucket_tiles.reshape(turn_count, batch_size, tile_size, tile_size),
        ),
    )
    row_max = row_max.reshape(slot_count, head_count, tile_size)
    row_sum = row_sum.reshape(slot_count, head_count, tile_size)
    weighted = weighted.reshape(slot_count, tile_size, head_count, head_dim)
    member = query_block[None, :] == query_ids[:, None]
    chosen = member.astype(jnp.float32)
    block_max = jnp.max(jnp.where(member[:, :, None, None], row_max[None], LOW_FLOOR), axis=1)
    slot_max = jnp.einsum("qs,qhi->shi", chosen, block_max, precision=lax.Precision.HIGHEST)
    slot_live = (query_block >= 0)[:, None, None]
    factor = jnp.where(slot_live, jnp.exp(jnp.where(slot_live, row_max - slot_max, 0.0)), 0.0)
    block_sum = jnp.einsum("qs,shi->qih", chosen, factor * row_sum, precision=lax.Precision.HIGHEST)
    block_out = jnp.einsum(
        "qs,sihd->qihd",
        chosen,
        jnp.transpose(factor, (0, 2, 1))[..., None] * weighted,
        precision=lax.Precision.HIGHEST,
    )
    range_rows = query_count * tile_size
    max_rows = jnp.transpose(block_max, (0, 2, 1)).reshape(range_rows, head_count)
    sum_rows = block_sum.reshape(range_rows, head_count)
    out_rows = block_out.reshape(range_rows, head_count, head_dim)
    col_max, col_sum, col_out = (
        lax.all_to_all(max_rows[None], "col", split_axis=1, concat_axis=0, tiled=True),
        lax.all_to_all(sum_rows[None], "col", split_axis=1, concat_axis=0, tiled=True),
        lax.all_to_all(out_rows[None], "col", split_axis=1, concat_axis=0, tiled=True),
    )
    global_max = jnp.max(col_max, axis=0)
    col_factor = jnp.exp(col_max - global_max[None])
    mine_sum = jnp.sum(col_factor * col_sum, axis=0)
    mine_out = jnp.sum(col_factor[..., None] * col_out, axis=0)
    attention = (mine_out / mine_sum[..., None]).reshape(rows_own, model_width).astype(jnp.bfloat16)
    update = jnp.dot(attention, w_out, preferred_element_type=jnp.float32)
    return (node_features.astype(jnp.float32) + update).astype(jnp.bfloat16)


def solution(mesh):
    return jax.shard_map(
        local,
        mesh=mesh,
        in_specs=(
            P(("row", "col"), None),
            P(),
            P(),
            P(),
            P(),
            P(),
            P(),
            P("row", "col", None, None),
            P("row", "col", None, None, None),
            P("row", "col", None, None, None, None),
        ),
        out_specs=P(("row", "col"), None),
        check_vma=False,
    )
```

profile of v0, /device:TPU:15, one launch (start us, length us, event | category | flops | bytes accessed | tf_op | source)
XLA Modules:
  0.0 311.0 jit_solution(13089731285216129570)
XLA Ops:
  9.0 3.9 %convolution_convert_fusion.2 = bf16[128,2048]{1,0:T(8,128)(2,1)} fusion(bf16[1024,2048]{1,0:T(8,128)(2,1)} %param.15, bf16[128,1024]{1,0:T(8,128)(2,1)} %param.12, f32[1024]{0:T(1024)} %param.13, f32[128]{0:T(128)S(1)} %add_rsqrt_fusion, f32[128]{0:T(128)S(1)} %broadcast_multiply_fusion), kind=kOutput, calls=%fused_computation.37 | convolution fusion | flops 537788416 | bytes 4985856 | tf_op jit(solution)/shard_map/dot_general | solution.py:39
  15.3 4.3 %all-to-all-start = ((bf16[1,1,4,4,128,128]{4,5,3,1,0,2:T(8,128)(2,1)}), bf16[1,1,4,4,128,128]{4,5,3,1,0,2:T(8,128)(2,1)}, u32[]{:S(2)}, u32[]{:S(2)}) async-start(bf16[1,1,4,4,128,128]{4,5,3,1,0,2:T(8,128)(2,1)} %copy.100), calls=%async_computation | async-start | bytes 1048576 | tf_op jit(solution)/shard_map/all_to_all | solution.py:43
  19.8 31.7 %all-gather.5.cloned.1.call-done = bf16[512,2048]{1,0:T(8,128)(2,1)} async-done(((bf16[128,2048]{1,0:T(8,128)(2,1)}), bf16[512,2048]{1,0:T(8,128)(2,1)}) %all-gather.5.cloned.1.call-update) | async-done | bytes 2097168 | tf_op jit(solution)/shard_map/all_gather | solution.py:42
  51.5 4.6 %reshape.131 = bf16[4,262144]{1,0:T(4,128)(2,1)} reshape(bf16[512,2048]{1,0:T(8,128)(2,1)} %all-gather.5.cloned.1.call-done) | data formatting | bytes 4194304 | tf_op jit(solution)/shard_map/reshape | solution.py:55
  56.1 27.6 %all-gather.3.cloned.1.call-done = bf16[1024,1024]{1,0:T(8,128)(2,1)} async-done(((bf16[128,1024]{1,0:T(8,128)(2,1)}), bf16[1024,1024]{1,0:T(8,128)(2,1)}) %all-gather.3.cloned.1.call-update) | async-done | bytes 2097168 | tf_op jit(solution)/shard_map/all_gather | solution.py:38
  83.7 3.8 %reshape.130 = bf16[8,131072]{1,0:T(8,128)(2,1)} reshape(bf16[1024,1024]{1,0:T(8,128)(2,1)} %all-gather.3.cloned.1.call-done) | data formatting | bytes 4194304 | tf_op jit(solution)/shard_map/reshape | solution.py:53
  87.6 80.1 %while.15 = (s32[]{:T(128)}, f32[4,4,8,128]{3,1,0,2:T(4,128)S(1)}, f32[4,4,8,128]{3,1,0,2:T(4,128)}, f32[4,4,128,8,128]{2,4,3,1,0:T(8,128)}, s32[4,4]{1,0:T(4,12...) while((s32[]{:T(128)}, f32[4,4,8,128]{3,1,0,2:T(4,128)S(1)}, ...), condition=%wide.region_5.6_spmd.clone, body=%wide.region_2.5_spmd.clone.sunk | while | flops 496033856 | bytes 54004036 | solution.py:100
  87.6 2.9 fusion.71
  93.1 2.6 fusion.69
  97.6 2.5 fusion.74
  103.6 3.0 bitcast_dynamic-update-slice_fusion.2
  107.6 2.9 fusion.71
  113.1 2.6 fusion.69
  117.6 2.5 fusion.74
  123.7 3.0 bitcast_dynamic-update-slice_fusion.2
  127.6 2.9 fusion.71
  133.1 2.6 fusion.69
  137.6 2.5 fusion.74
  143.7 3.0 bitcast_dynamic-update-slice_fusion.2
  147.7 2.9 fusion.71
  153.2 2.6 fusion.69
  157.7 2.5 fusion.74
  163.7 3.0 bitcast_dynamic-update-slice_fusion.2
  172.8 3.7 %all-to-all-start.3 = ((f32[8,1,1024]{2,1,0:T(1,128)}), f32[8,1,1024]{2,1,0:T(1,128)S(1)}, u32[]{:S(2)}, u32[]{:S(2)}) async-start(f32[8,1,1024]{2,1,0:T(1,128)} %reshape.155), calls=%async_computation.3 | async-start | bytes 65536 | tf_op jit(solution)/shard_map/all_to_all | solution.py:131
  176.7 1.9 reduce.10
  179.8 9.2 %copy.109 = f32[16,128,8,128]{3,0,2,1:T(8,128)} copy(f32[16,128,8,128]{1,3,2,0:T(8,128)} %bitcast.122) | data formatting | bytes 16777216 | tf_op jit(solution)/shard_map/reshape | solution.py:111
  189.0 5.1 %all-to-all-start.1 = ((f32[8,1,1024]{2,1,0:T(1,128)}), f32[8,1,1024]{2,1,0:T(1,128)S(1)}, u32[]{:S(2)}, u32[]{:S(2)}) async-start(f32[8,1,1024]{2,1,0:T(1,128)} %reshape.153), calls=%async_computation.1 | async-start | bytes 65536 | tf_op jit(solution)/shard_map/all_to_all | solution.py:130
  194.1 7.4 %fusion.19 = f32[8,128,8,128]{3,0,2,1:T(8,128)S(1)} fusion(f32[16,128,8,128]{3,0,2,1:T(8,128)} %copy.109, f32[16,128,8]{0,2,1:T(8,128)S(1)} %copy.108, s32[16]{0:T(128)S(1)} %get-tuple-element.149), kind=kOutput, calls=%fused_computation.33 | convolution fusion | flops 203423872 | bytes 12648512 | tf_op jit(solution)/shard_map/qs,sihd->qihd/dot_general | solution.py:119
  201.5 2.7 copy.110
  204.2 5.1 %all-to-all-start.2 = ((f32[1,1024,8,128]{3,2,0,1:T(8,128)}), f32[1,1024,8,128]{3,2,0,1:T(8,128)}, u32[]{:S(2)}, u32[]{:S(2)}) async-start(f32[1,1024,8,128]{3,2,0,1:T(8,128)} %bitcast.121), calls=%async_computation.2 | async-start | bytes 8388608 | tf_op jit(solution)/shard_map/all_to_all | solution.py:132
  213.2 86.6 %all-to-all-done.2 = f32[1,1024,8,128]{3,2,0,1:T(8,128)} async-done(((f32[1,1024,8,128]{3,2,0,1:T(8,128)}), f32[1,1024,8,128]{3,2,0,1:T(8,128)}, u32[]{:S(2)}, u32[]{:S(2)}) %all-to-all-start.2) | async-done | bytes 4194336 | tf_op jit(solution)/shard_map/all_to_all | solution.py:132
  299.8 3.0 multiply_reduce_fusion
  (128 shorter events, 52.4 us)
Async XLA Ops:
  6.5 6.4 %copy-start = (bf16[1024,1024]{1,0:T(8,128)(2,1)S(1)}, bf16[1024,1024]{1,0:T(8,128)(2,1)}, u32[]{:S(2)}) copy-start(bf16[1024,1024]{1,0:T(8,128)(2,1)} %param.14) | copy-start | bytes 6291460
  6.5 44.9 %all-gather.5.cloned.1.call-start = ((), (), s32[]{:S(2)}) async-start(), calls=%async_computation.5 | async-start | bytes 2621440 | tf_op jit(solution)/shard_map/all_gather | solution.py:42
  8.9 4.1 %copy-start.4 = (bf16[128,1024]{1,0:T(8,128)(2,1)S(1)}, bf16[128,1024]{1,0:T(8,128)(2,1)}, u32[]{:S(2)}) copy-start(bf16[128,1024]{1,0:T(8,128)(2,1)} %param.12) | copy-start | bytes 786436
  9.0 4.1 %copy-start.8 = (f32[1024]{0:T(1024)S(1)}, f32[1024]{0:T(1024)}, u32[]{:S(2)}) copy-start(f32[1024]{0:T(1024)} %param.13) | copy-start | bytes 12292
  12.9 1.3 copy-start.6
  12.9 6.7 %copy-start.10 = (s32[1,1,2,16]{3,2,1,0:T(2,128)S(1)}, s32[1,1,2,16]{3,2,1,0:T(2,128)}, u32[]{:S(2)}) copy-start(s32[1,1,2,16]{3,2,1,0:T(2,128)} %param.19) | copy-start | bytes 388
  12.9 70.8 %all-gather.3.cloned.1.call-start = ((), (), s32[]{:S(2)}) async-start(), calls=%async_computation.4 | async-start | bytes 2359296 | tf_op jit(solution)/shard_map/all_gather | solution.py:38
  15.3 72.3 %all-to-all-start = ((bf16[1,1,4,4,128,128]{4,5,3,1,0,2:T(8,128)(2,1)}), bf16[1,1,4,4,128,128]{4,5,3,1,0,2:T(8,128)(2,1)}, u32[]{:S(2)}, u32[]{:S(2)}) async-start(bf16[1,1,4,4,128,128]{4,5,3,1,0,2:T(8,128)(2,1)} %copy.100), calls=%async_computation | async-start | bytes 1048576 | tf_op jit(solution)/shard_map/all_to_all | solution.py:43
  56.1 31.5 %copy-start.7 = (f32[32,8]{0,1:T(8,128)S(1)}, f32[32,8]{0,1:T(8,128)}, u32[]{:S(2)}) copy-start(f32[32,8]{0,1:T(8,128)} %param.17) | copy-start | bytes 3076
  56.1 31.5 %copy-start.9 = (f32[8]{0:T(128)S(1)}, f32[8]{0:T(128)}, u32[]{:S(2)}) copy-start(f32[8]{0:T(128)} %param.18) | copy-start | bytes 100
  97.6 3.6 %copy-start.2 = (f32[4,128,128,8]{1,2,3,0:T(8,128)S(1)}, f32[4,128,128,8]{1,2,3,0:T(8,128)}, u32[]{:S(2)}) copy-start(f32[4,128,128,8]{1,2,3,0:T(8,128)} %copy.161) | copy-start | bytes 6291460 | tf_op jit(solution)/shard_map/while
  97.6 3.6 %copy-start.3 = (bf16[4,128,1,8,128]{4,3,2,1,0:T(8,128)(2,1)S(1)}, bf16[4,128,1,8,128]{4,3,2,1,0:T(8,128)(2,1)}, u32[]{:S(2)}) copy-start(bf16[4,128,1,8,128]{4,3,2,1,0:T(8,128)(2,1)} %get-tuple-element.229) | copy-start | bytes 3145732 | tf_op jit(solution)/shard_map/while
  117.6 3.6 %copy-start.2 = (f32[4,128,128,8]{1,2,3,0:T(8,128)S(1)}, f32[4,128,128,8]{1,2,3,0:T(8,128)}, u32[]{:S(2)}) copy-start(f32[4,128,128,8]{1,2,3,0:T(8,128)} %copy.161) | copy-start | bytes 6291460 | tf_op jit(solution)/shard_map/while
  117.6 3.6 %copy-start.3 = (bf16[4,128,1,8,128]{4,3,2,1,0:T(8,128)(2,1)S(1)}, bf16[4,128,1,8,128]{4,3,2,1,0:T(8,128)(2,1)}, u32[]{:S(2)}) copy-start(bf16[4,128,1,8,128]{4,3,2,1,0:T(8,128)(2,1)} %get-tuple-element.229) | copy-start | bytes 3145732 | tf_op jit(solution)/shard_map/while
  137.6 3.6 %copy-start.2 = (f32[4,128,128,8]{1,2,3,0:T(8,128)S(1)}, f32[4,128,128,8]{1,2,3,0:T(8,128)}, u32[]{:S(2)}) copy-start(f32[4,128,128,8]{1,2,3,0:T(8,128)} %copy.161) | copy-start | bytes 6291460 | tf_op jit(solution)/shard_map/while
  137.6 3.6 %copy-start.3 = (bf16[4,128,1,8,128]{4,3,2,1,0:T(8,128)(2,1)S(1)}, bf16[4,128,1,8,128]{4,3,2,1,0:T(8,128)(2,1)}, u32[]{:S(2)}) copy-start(bf16[4,128,1,8,128]{4,3,2,1,0:T(8,128)(2,1)} %get-tuple-element.229) | copy-start | bytes 3145732 | tf_op jit(solution)/shard_map/while
  157.7 3.6 %copy-start.2 = (f32[4,128,128,8]{1,2,3,0:T(8,128)S(1)}, f32[4,128,128,8]{1,2,3,0:T(8,128)}, u32[]{:S(2)}) copy-start(f32[4,128,128,8]{1,2,3,0:T(8,128)} %copy.161) | copy-start | bytes 6291460 | tf_op jit(solution)/shard_map/while
  157.7 3.6 %copy-start.3 = (bf16[4,128,1,8,128]{4,3,2,1,0:T(8,128)(2,1)S(1)}, bf16[4,128,1,8,128]{4,3,2,1,0:T(8,128)(2,1)}, u32[]{:S(2)}) copy-start(bf16[4,128,1,8,128]{4,3,2,1,0:T(8,128)(2,1)} %get-tuple-element.229) | copy-start | bytes 3145732 | tf_op jit(solution)/shard_map/while
  172.8 16.2 %all-to-all-start.3 = ((f32[8,1,1024]{2,1,0:T(1,128)}), f32[8,1,1024]{2,1,0:T(1,128)S(1)}, u32[]{:S(2)}, u32[]{:S(2)}) async-start(f32[8,1,1024]{2,1,0:T(1,128)} %reshape.155), calls=%async_computation.3 | async-start | bytes 65536 | tf_op jit(solution)/shard_map/all_to_all | solution.py:131
  189.0 15.2 %all-to-all-start.1 = ((f32[8,1,1024]{2,1,0:T(1,128)}), f32[8,1,1024]{2,1,0:T(1,128)S(1)}, u32[]{:S(2)}, u32[]{:S(2)}) async-start(f32[8,1,1024]{2,1,0:T(1,128)} %reshape.153), calls=%async_computation.1 | async-start | bytes 65536 | tf_op jit(solution)/shard_map/all_to_all | solution.py:130
  204.2 95.6 %all-to-all-start.2 = ((f32[1,1024,8,128]{3,2,0,1:T(8,128)}), f32[1,1024,8,128]{3,2,0,1:T(8,128)}, u32[]{:S(2)}, u32[]{:S(2)}) async-start(f32[1,1024,8,128]{3,2,0,1:T(8,128)} %bitcast.121), calls=%async_computation.2 | async-start | bytes 8388608 | tf_op jit(solution)/shard_map/all_to_all | solution.py:132
  299.8 3.3 %copy-start.5 = (bf16[1024,1024]{1,0:T(8,128)(2,1)S(1)}, bf16[1024,1024]{1,0:T(8,128)(2,1)}, u32[]{:S(2)}) copy-start(bf16[1024,1024]{1,0:T(8,128)(2,1)} %param.16) | copy-start | bytes 6291460
  299.8 4.4 %copy-start.1 = (bf16[1024,1024]{1,0:T(8,128)(2,1)S(1)}, bf16[1024,1024]{1,0:T(8,128)(2,1)}, u32[]{:S(2)}) copy-start(bf16[1024,1024]{1,0:T(8,128)(2,1)} %param.14) | copy-start | bytes 6291460
Sparse Core Ops, SparseCore 0:
  13.0 38.3 all-gather.4
  53.1 30.6 all-gather.2
where the time goes:
time: 317 us; the launch traced here: 311 us
  waiting for transfers between devices  146 us (46%)
  matrix products  62.6 us (20%)
  local copies, waits for them, and re-layouts  54 us (17%)
  starting transfers between devices  18.3 us (6%)
  other arithmetic  16.3 us (5%)
  between operations  13.6 us (4%)
    all_to_all x1, waiting for transfers between devices, local(): lax.all_to_all(out_rows[None], 'col', split_axis=1, concat_axis=0, tiled=...  86.6 us
    all_gather x1, waiting for transfers between devices, local(): key_group = lax.all_gather(key_value, 'row', axis=0, tiled=True)  31.7 us
    all_gather x1, waiting for transfers between devices, local(): query_range = lax.all_gather(queries, 'col', axis=0, tiled=True)  27.6 us
    dot_general x4, matrix products, score_slots(): jnp.einsum('shij,sjhd->sihd', prob_vals, value_sel, preferred_element_typ...  12 us
    dot_general x4, matrix products, score_slots(): jnp.dot(key_pick, key_flat, preferred_element_type=jnp.float32)  11.5 us
    dot_general x4, matrix products, score_slots(): jnp.einsum('sijb,bh->shij', bucket_hot, bias_table, precision=lax.Precisi...  10.4 us
    dot_general x4, matrix products, score_slots(): jnp.dot(query_pick, query_flat, preferred_element_type=jnp.float32)  9.99 us
    reshape x1, local copies, waits for them, and re-layouts, local(): weighted = weighted.reshape(slot_count, tile_size, head_count, head_dim)  9.18 us
  transfers between devices with their start and end apart: 6, of which 3 were waited for; matrix products, arithmetic and copies ran while one was open for 12% of the time, Pallas kernels for 0%

commit v1 on v0

v1 whole, which is shorter than its diff:
```python
import functools

import jax
import jax.numpy as jnp
from jax import lax
from jax.experimental import pallas as pl
from jax.experimental.pallas import tpu as pltpu
from jax.sharding import PartitionSpec as P

EPSILON = 1e-05
LOW_FLOOR = -1e30
CORES = 2
MESH = pl.DeviceIdType.MESH
VMEM_LIMIT = 60 * 2**20


def normalize(features, gain_vec):
    as_float = features.astype(jnp.float32)
    centered = as_float - jnp.mean(as_float, axis=-1, keepdims=True)
    variance = jnp.mean(centered * centered, axis=-1, keepdims=True)
    return (centered * lax.rsqrt(variance + EPSILON) * gain_vec).astype(jnp.bfloat16)


def greet(partners):
    barrier = pltpu.get_barrier_semaphore()
    for partner in partners:
        pl.semaphore_signal(barrier, inc=1, device_id=partner, device_id_type=MESH)
    pl.semaphore_wait(barrier, len(partners))


def exchange(n_row, n_chip, q_in, n_in, e_in, q_out, n_out, e_out, send_sem, recv_sem, own_sem):
    row, col = lax.axis_index("row"), lax.axis_index("col")
    chip, core = col // CORES, col % CORES
    sibling = (row, chip * CORES + (1 - core))
    chips = [(row, ((chip + k) % n_chip) * CORES + core) for k in range(1, n_chip)]
    rows = [((row + k) % n_row, col) for k in range(1, n_row)]
    greet(chips + [sibling] + rows)
    count = [0]

    def send(src, dst, where):
        spot = count[0]
        count[0] += 1
        copy = pltpu.make_async_remote_copy(
            src_ref=src,
            dst_ref=dst,
            send_sem=send_sem.at[spot],
            recv_sem=recv_sem.at[spot],
            device_id=where,
            device_id_type=MESH,
        )
        copy.start()
        return copy

    over_chips = [send(q_in, q_out.at[col], where) for where in chips]
    rest = [send(n_in, n_out.at[row], where) for where in rows]
    rest += [send(e_in.at[where[0]], e_out.at[row], where) for where in rows]
    rest.append(send(q_in, q_out.at[col], sibling))
    own = [
        pltpu.make_async_copy(q_in, q_out.at[col], own_sem.at[0]),
        pltpu.make_async_copy(n_in, n_out.at[row], own_sem.at[1]),
        pltpu.make_async_copy(e_in.at[row], e_out.at[row], own_sem.at[2]),
    ]
    for copy in own:
        copy.start()
    for k, copy in enumerate(over_chips, 1):
        copy.wait_recv()
        origin = ((chip + n_chip - k) % n_chip) * CORES + core
        rest.append(send(q_out.at[origin], q_out.at[origin], sibling))
    for copy in over_chips:
        copy.wait_send()
    for copy in rest:
        copy.wait()
    for copy in own:
        copy.wait()


def attend(
    slot_cap, scale, pairs, slope, table, q_ref, kv_ref, e_ref, b_ref, o_ref, l_ref, m_acc, s_acc, o_acc
):
    query_count, tile, width = q_ref.shape
    heads = l_ref.shape[1]
    dim = width // heads
    m_acc[...] = jnp.full(m_acc.shape, LOW_FLOOR, jnp.float32)
    s_acc[...] = jnp.zeros(s_acc.shape, jnp.float32)
    o_acc[...] = jnp.zeros(o_acc.shape, jnp.float32)
    ones = jnp.ones((tile, dim), jnp.bfloat16)

    def slot_step(slot, carry):
        query = pairs[0, slot]

        @pl.when(query >= 0)
        def _():
            key = pairs[1, slot] + slot // slot_cap
            buckets = b_ref[slot]
            edges = e_ref[slot].astype(jnp.float32)
            for h in range(heads):
                cols = slice(h * dim, (h + 1) * dim)
                vals = slice(width + h * dim, width + (h + 1) * dim)
                score = lax.dot_general(
                    q_ref[query, :, cols],
                    kv_ref[key, :, cols],
                    (((1,), (1,)), ((), ())),
                    preferred_element_type=jnp.float32,
                )
                entries = jnp.broadcast_to(table[h : h + 1, :], (tile, table.shape[1]))
                bias = jnp.take_along_axis(entries, buckets, axis=1, mode="promise_in_bounds")
                score = score * scale + bias + slope[h] * edges
                old_max = m_acc[query, h]
                new_max = jnp.maximum(old_max, jnp.max(score, axis=-1, keepdims=True))
                probs = jnp.exp(score - new_max).astype(jnp.bfloat16)
                both = jnp.dot(
                    probs,
                    jnp.concatenate([kv_ref[key, :, vals], ones], axis=1),
                    preferred_element_type=jnp.float32,
                )
                keep = jnp.exp(old_max - new_max)
                m_acc[query, h] = new_max
                o_acc[query, h] = o_acc[query, h] * keep + both[:, :dim]
                s_acc[query, h] = s_acc[query, h] * keep + both[:, dim:]

        return carry

    lax.fori_loop(0, pairs.shape[1], slot_step, 0)
    lane = lax.broadcasted_iota(jnp.int32, (tile, tile), 1)

    def finish(query, carry):
        packed = jnp.full((tile, tile), LOW_FLOOR, jnp.float32)
        for h in range(heads):
            total = s_acc[query, h]
            live = total > 0.0
            safe = jnp.where(live, total, 1.0)
            o_ref[query, :, h * dim : (h + 1) * dim] = (o_acc[query, h] / safe).astype(o_ref.dtype)
            level = jnp.where(live, m_acc[query, h] + jnp.log(safe), LOW_FLOOR)
            packed = jnp.where(lane == h, level, packed)
        l_ref[query] = packed.T[:heads]
        return carry

    lax.fori_loop(0, query_count, finish, 0)


def blend(levels, parts, heads):
    top = functools.reduce(jnp.maximum, levels)
    shares = [jnp.exp(level - top) for level in levels]
    total = functools.reduce(jnp.add, shares)
    weights = [(share / total).T for share in shares]
    dim = parts[0].shape[1] // heads
    out = []
    for h in range(heads):
        cols = slice(h * dim, (h + 1) * dim)
        terms = [w[:, h : h + 1] * part[:, cols].astype(jnp.float32) for w, part in zip(weights, parts)]
        out.append(functools.reduce(jnp.add, terms))
    return out, top + jnp.log(total)


def combine(
    n_chip, o_ref, l_ref, a_ref, sib_o, sib_l, mix_o, mix_l, got_o, got_l, send_sem, recv_sem
):
    row, col = lax.axis_index("row"), lax.axis_index("col")
    chip, core = col // CORES, col % CORES
    heads = l_ref.shape[1]
    dim = o_ref.shape[2] // heads
    sibling = (row, chip * CORES + (1 - core))
    chips = [(row, ((chip + k) % n_chip) * CORES + core) for k in range(1, n_chip)]
    greet(chips + [sibling])

    def send(spot, src, dst, where):
        copy = pltpu.make_async_remote_copy(
            src_ref=src,
            dst_ref=dst,
            send_sem=send_sem.at[spot],
            recv_sem=recv_sem.at[spot],
            device_id=where,
            device_id_type=MESH,
        )
        copy.start()
        return copy

    order = list(range(1, n_chip)) + [0]
    to_sibling = {}
    for k in order:
        theirs = ((chip + k) % n_chip) * CORES + (1 - core)
        to_sibling[k] = [
            send(4 * k, l_ref.at[theirs], sib_l.at[k], sibling),
            send(4 * k + 1, o_ref.at[theirs], sib_o.at[k], sibling),
        ]
    over = []

    def push(k):
        over.append(send(4 * k + 2, mix_l.at[k], got_l.at[k], chips[k - 1]))
        over.append(send(4 * k + 3, mix_o.at[k], got_o.at[k], chips[k - 1]))

    for k in range(1, n_chip):
        for copy in to_sibling[k]:
            copy.wait_recv()
        mine = ((chip + k) % n_chip) * CORES + core
        out, level = blend([l_ref[mine], sib_l[k]], [o_ref[mine], sib_o[k]], heads)
        for h in range(heads):
            mix_o[k, :, h * dim : (h + 1) * dim] = out[h].astype(mix_o.dtype)
        mix_l[k] = level
        push(k)
    for copy in to_sibling[0]:
        copy.wait_recv()
    for copy in over:
        copy.wait_recv()
    levels = [l_ref[col], sib_l[0]] + [got_l[k] for k in range(1, n_chip)]
    parts = [o_ref[col], sib_o[0]] + [got_o[k] for k in range(1, n_chip)]
    out, _ = blend(levels, parts, heads)
    for h in range(heads):
        a_ref[:, h * dim : (h + 1) * dim] = out[h].astype(a_ref.dtype)
    for copies in to_sibling.values():
        for copy in copies:
            copy.wait_send()
    for copy in over:
        copy.wait_send()


def local(
    n_row,
    n_col,
    node_features,
    norm_gain,
    w_query,
    w_keyvalue,
    w_out,
    bias_table,
    edge_slope,
    pair_blocks,
    bucket_ids,
    edge_weight,
):
    tile, width = node_features.shape
    heads = edge_slope.shape[0]
    dim = width // heads
    n_chip = n_col // CORES
    slot_cap = edge_weight.shape[3]
    slots = n_row * slot_cap
    bf16, f32 = jnp.bfloat16, jnp.float32
    vmem = pl.BlockSpec(memory_space=pltpu.VMEM)
    smem = pl.BlockSpec(memory_space=pltpu.SMEM)
    hbm = pl.BlockSpec(memory_space=pl.ANY)

    normalized = normalize(node_features, norm_gain)
    queries = jnp.dot(normalized, w_query, preferred_element_type=f32).astype(bf16)
    copies = 2 * (n_chip - 1) + 2 * (n_row - 1) + 1
    query_range, norm_group, edge_values = pl.pallas_call(
        functools.partial(exchange, n_row, n_chip),
        out_shape=(
            jax.ShapeDtypeStruct((n_col, tile, width), bf16),
            jax.ShapeDtypeStruct((n_row, tile, width), bf16),
            jax.ShapeDtypeStruct((n_row,) + edge_weight.shape[3:], edge_weight.dtype),
        ),
        in_specs=[vmem] * 3,
        out_specs=(hbm,) * 3,
        scratch_shapes=[
            pltpu.SemaphoreType.DMA((copies,)),
            pltpu.SemaphoreType.DMA((copies,)),
            pltpu.SemaphoreType.DMA((3,)),
        ],
        compiler_params=pltpu.CompilerParams(collective_id=0, has_side_effects=True),
        name="exchange",
    )(queries, normalized, edge_weight[0, 0])
    key_value = jnp.dot(
        norm_group.reshape(n_row * tile, width), w_keyvalue, preferred_element_type=f32
    ).astype(bf16)
    table = jnp.pad(bias_table.T, ((0, 0), (0, tile - bias_table.shape[0])))
    partial_out, partial_level = pl.pallas_call(
        functools.partial(attend, slot_cap, dim ** (-0.5)),
        out_shape=(
            jax.ShapeDtypeStruct((n_col, tile, width), bf16),
            jax.ShapeDtypeStruct((n_col, heads, tile), f32),
        ),
        in_specs=[smem, smem] + [vmem] * 5,
        out_specs=(vmem, vmem),
        scratch_shapes=[pltpu.VMEM((n_col, heads, tile, tile), f32)] * 2
        + [pltpu.VMEM((n_col, heads, tile, dim), f32)],
        compiler_params=pltpu.CompilerParams(vmem_limit_bytes=VMEM_LIMIT),
        name="attend",
    )(
        pair_blocks.reshape(2, slots),
        edge_slope,
        table,
        query_range,
        key_value.reshape(n_row, tile, 2 * width),
        edge_values.reshape(slots, tile, tile),
        bucket_ids.reshape(slots, tile, tile),
    )
    attention = pl.pallas_call(
        functools.partial(combine, n_chip),
        out_shape=jax.ShapeDtypeStruct((tile, width), bf16),
        in_specs=[vmem] * 2,
        out_specs=vmem,
        scratch_shapes=[
            pltpu.VMEM((n_chip, tile, width), bf16),
            pltpu.VMEM((n_chip, heads, tile), f32),
        ]
        * 3
        + [pltpu.SemaphoreType.DMA((4 * n_chip,))] * 2,
        compiler_params=pltpu.CompilerParams(
            collective_id=1, has_side_effects=True, vmem_limit_bytes=VMEM_LIMIT
        ),
        name="combine",
    )(partial_out, partial_level)
    update = jnp.dot(attention, w_out, preferred_element_type=f32)
    return (node_features.astype(f32) + update).astype(bf16)


def solution(mesh):
    return jax.shard_map(
        functools.partial(local, mesh.shape["row"], mesh.shape["col"]),
        mesh=mesh,
        in_specs=(
            P(("row", "col"), None),
            P(),
            P(),
            P(),
            P(),
            P(),
            P(),
            P("row", "col", None, None),
            P("row", "col", None, None, None),
            P("row", "col", None, None, None, None),
        ),
        out_specs=P(("row", "col"), None),
        check_vma=False,
    )
```

time: 317 us -> 115 us (0.36); the launches traced: 311 us -> 115 us
  waiting for transfers between devices: 146 us -> 0 us
  Pallas kernels: 0 us -> 100 us
  local copies, waits for them, and re-layouts: 54 us -> 1.3 us
  matrix products: 62.6 us -> 10.1 us
  starting transfers between devices: 18.3 us -> 0 us
  between operations: 13.6 us -> 0.06 us
  other arithmetic: 16.3 us -> 3.57 us
    pallas_call x0 -> x3, Pallas kernels: none -> 100 us  [the longest x1 40.9 us: local(): pl.pallas_call(functools.partial(combine, n_chip), out_shape=jax.ShapeDty...]
    all_to_all x4 -> x0, waiting for transfers between devices: 86.6 us -> none  [the longest x1 86.6 us: local(): lax.all_to_all(out_rows[None], 'col', split_axis=1, concat_axis=0, tiled=...]
    all_gather x2 -> x0, waiting for transfers between devices: 59.3 us -> none  [the longest x1 31.7 us: local(): key_group = lax.all_gather(key_value, 'row', axis=0, tiled=True)]
    dot_general x26 -> x3, matrix products: 62.6 us -> 10.1 us  [the longest x1 6.15 us: local(): jnp.dot(norm_group.reshape(n_row * tile, width), w_keyvalue, preferred_el...]
    all_to_all x4 -> x0, starting transfers between devices: 18.2 us -> none  [the longest x1 5.12 us: local(): lax.all_to_all(max_rows[None], 'col', split_axis=1, concat_axis=0, tiled=...]
    reshape x3 -> x0, local copies, waits for them, and re-layouts: 17.6 us -> none  [the longest x1 9.18 us: local(): weighted = weighted.reshape(slot_count, tile_size, head_count, head_dim)]
    dot_general x5 -> x0, local copies, waits for them, and re-layouts: 10.1 us -> none  [the longest x4 7.44 us: score_slots(): jnp.einsum('sijb,bh->shij', bucket_hot, bias_table, precision=lax.Precisi...]
    while x28 -> x0, local copies, waits for them, and re-layouts: 7.73 us -> none
  transfers between devices with their start and end apart: 6 -> 0, of which waited for: 3 -> 0; matrix products, arithmetic and copies ran while one was open for 12% -> 0% of each run, Pallas kernels for 0% -> 0%
where the time goes in v1:
time: 115 us
  Pallas kernels  100 us (87%)
  matrix products  10.1 us (9%)
  other arithmetic  3.57 us (3%)
  local copies, waits for them, and re-layouts  1.3 us (1%)
    pallas_call x1, Pallas kernels, local(): pl.pallas_call(functools.partial(combine, n_chip), out_shape=jax.ShapeDty...  40.9 us
    pallas_call x1, Pallas kernels, local(): pl.pallas_call(functools.partial(attend, slot_cap, dim ** (-0.5)), out_sh...  29.7 us
    pallas_call x1, Pallas kernels, local(): pl.pallas_call(functools.partial(exchange, n_row, n_chip), out_shape=(jax...  29.7 us
    dot_general x1, matrix products, local(): jnp.dot(norm_group.reshape(n_row * tile, width), w_keyvalue, preferred_el...  6.15 us
    dot_general x1, matrix products, local(): update = jnp.dot(attention, w_out, preferred_element_type=f32)  2.84 us

profile of v1, /device:TPU:15, one launch (start us, length us, event | category | flops | bytes accessed | tf_op | source)
XLA Modules:
  0.0 115.4 jit_solution(11685505230049014193)
XLA Ops:
  0.0 0.0 copy-start
  0.0 1.2 %convert_reduce_fusion = f32[128]{0:T(128)S(1)} fusion(bf16[128,1024]{1,0:T(8,128)(2,1)} %param.10), kind=kLoop, calls=%fused_computation.5 | loop fusion | flops 262016 | bytes 262656 | tf_op jit(solution)/shard_map/reduce_sum | solution.py:19
  1.2 1.2 %fusion.3 = f32[128]{0:T(128)S(1)} fusion(bf16[128,1024]{1,0:T(8,128)(2,1)} %param.10, f32[128]{0:T(128)S(1)} %broadcast_multiply_fusion), kind=kLoop, calls=%fused_computation.8 | loop fusion | flops 524160 | bytes 263168 | tf_op jit(solution)/shard_map/reduce_sum | solution.py:20
  2.4 1.3 %pad.4.table = f32[8,128]{1,0:T(8,128)} pad(f32[8,32]{1,0:T(8,128)} %bitcast.17, f32[]{:T(128)} %constant.3.clone.1), padding=0_0x0_96 | pad | bytes 5124 | tf_op jit(solution)/shard_map/jit(_pad)/pad | solution.py:265
  3.7 1.2 %fusion.5.n_in = bf16[128,1024]{1,0:T(8,128)(2,1)S(1)} fusion(bf16[128,1024]{1,0:T(8,128)(2,1)} %param.10, f32[1024]{0:T(1024)} %param.11, f32[128]{0:T(128)S(1)} %add_rsqrt_fusion, f32[128]{0:T(128)S(1)} %broadcast_multiply_fusion), kind=kLoop, calls=%fused_computation.10 | loop fusion | flops 655360 | bytes 529408 | tf_op jit(solution)/shard_map/convert_element_type | solution.py:21
  4.9 0.0 copy-done
  4.9 0.0 copy-start.2
  4.9 1.2 convolution_convert_fusion.1.q_in
  6.0 0.0 copy-done.2
  6.1 29.7 %exchange.1 = (bf16[8,128,1024]{2,1,0:T(8,128)(2,1)}, bf16[4,128,1024]{2,1,0:T(8,128)(2,1)}, bf16[4,4,128,128]{3,2,1,0:T(8,128)(2,1)}) custom-call(bf16[128,1024]{1,0:T(8,128)(2,1)} %convolution_convert_fusion.1.q_in, bf16[128,1024]{1,0:T(8,128)(2,1)} %copy-done.2, bf16[4,4,128,128]{3,2,1,0:T(8,128)(2,1)} %bitcast.16), custom_call_target="tpu_custom_call" | custom-call | tf_op jit(solution)/shard_map/exchange/pallas_call | solution.py:245
  35.7 6.1 %convolution_convert_fusion = bf16[512,2048]{1,0:T(8,128)(2,1)} fusion(bf16[512,1024]{1,0:T(8,128)(2,1)} %bitcast.19, bf16[1024,2048]{1,0:T(8,128)(2,1)} %param.13), kind=kOutput, calls=%fused_computation | convolution fusion | flops 2148532224 | bytes 7340032 | tf_op jit(solution)/shard_map/dot_general | solution.py:262
  41.9 29.7 %attend.1 = (bf16[8,128,1024]{2,1,0:T(8,128)(2,1)}, f32[8,8,128]{2,1,0:T(8,128)}) custom-call(s32[2,16]{1,0:T(2,128)} %bitcast.18, f32[8]{0:T(128)} %slope.1, f32[8,128]{1,0:T(8,128)} %pad.4.table, bf16[8,128,1024]{2,1,0:T(8,128)(2,1)} %get-tuple-element.10.q_ref, bf16[4,128,2048]{2,1,0:T(8,128)(2,1)} %bitcast.13, bf16[16,128,128]{2,1,0:T(8,128)(2,1)} %bitcast.15, ...), custom_call_target="tpu_custom_call" | custom-call | tf_op jit(solution)/shard_map/attend/pallas_call | solution.py:266
  71.6 0.0 copy-start.1
  71.6 40.9 %combine.1 = bf16[128,1024]{1,0:T(8,128)(2,1)} custom-call(bf16[8,128,1024]{2,1,0:T(8,128)(2,1)} %get-tuple-element.13.o_ref, f32[8,8,128]{2,1,0:T(8,128)} %get-tuple-element.14.l_ref), custom_call_target="tpu_custom_call" | custom-call | tf_op jit(solution)/shard_map/combine/pallas_call | solution.py:287
  112.5 0.0 copy-done.1
  112.5 2.8 %fusion = bf16[128,1024]{1,0:T(8,128)(2,1)} fusion(bf16[128,1024]{1,0:T(8,128)(2,1)} %combine.1, bf16[1024,1024]{1,0:T(8,128)(2,1)} %param.14, bf16[128,1024]{1,0:T(8,128)(2,1)S(1)} %copy-done.1), kind=kOutput, calls=%fused_computation.3 | convolution fusion | flops 268828672 | bytes 2883584 | tf_op jit(solution)/shard_map/dot_general | solution.py:303
  (2 shorter events, 0.0 us)
Async XLA Ops:
  0.0 4.9 %copy-start = (bf16[1024,1024]{1,0:T(8,128)(2,1)S(1)}, bf16[1024,1024]{1,0:T(8,128)(2,1)}, u32[]{:S(2)}) copy-start(bf16[1024,1024]{1,0:T(8,128)(2,1)} %param.12) | copy-start | bytes 6291460
  4.9 1.2 %copy-start.2 = (bf16[128,1024]{1,0:T(8,128)(2,1)}, bf16[128,1024]{1,0:T(8,128)(2,1)S(1)}, u32[]{:S(2)}) copy-start(bf16[128,1024]{1,0:T(8,128)(2,1)S(1)} %fusion.5.n_in) | copy-start | bytes 786436
  71.6 40.9 %copy-start.1 = (bf16[128,1024]{1,0:T(8,128)(2,1)S(1)}, bf16[128,1024]{1,0:T(8,128)(2,1)}, u32[]{:S(2)}) copy-start(bf16[128,1024]{1,0:T(8,128)(2,1)} %param.10) | copy-start | bytes 786436

commit v2 on v1

v2 whole, which is shorter than its diff:
```python
import functools

import jax
import jax.numpy as jnp
from jax import lax
from jax.experimental import pallas as pl
from jax.experimental.pallas import tpu as pltpu
from jax.sharding import PartitionSpec as P

EPSILON = 1e-05
LOW_FLOOR = -1e30
CORES = 2
MESH = pl.DeviceIdType.MESH
LANES = 128
VMEM_LIMIT = 60 * 2**20


def normalize(features, gain_vec):
    as_float = features.astype(jnp.float32)
    centered = as_float - jnp.mean(as_float, axis=-1, keepdims=True)
    variance = jnp.mean(centered * centered, axis=-1, keepdims=True)
    return (centered * lax.rsqrt(variance + EPSILON) * gain_vec).astype(jnp.bfloat16)


def greet(partners):
    barrier = pltpu.get_barrier_semaphore()
    for partner in partners:
        pl.semaphore_signal(barrier, inc=1, device_id=partner, device_id_type=MESH)
    pl.semaphore_wait(barrier, len(partners))


def exchange(
    n_row, n_chip, q_in, n_in, e_in, w_in, q_out, k_out, v_out, e_out,
    n_buf, w_buf, send_sem, recv_sem, chip_sem, line_sem, own_sem,
):
    row, col = lax.axis_index("row"), lax.axis_index("col")
    chip, core = col // CORES, col % CORES
    sibling = (row, chip * CORES + (1 - core))
    chips = [(row, ((chip + k) % n_chip) * CORES + core) for k in range(1, n_chip)]
    rows = [((row + k) % n_row, col) for k in range(1, n_row)]
    width = n_in.shape[1]
    greet(chips + [sibling] + rows)

    def remote(src, dst, send, recv, where):
        return pltpu.make_async_remote_copy(
            src_ref=src,
            dst_ref=dst,
            send_sem=send,
            recv_sem=recv,
            device_id=where,
            device_id_type=MESH,
        )

    def hop(step, way):
        origin = chip - way * step
        spot = origin * CORES + core
        copy = remote(
            q_in if step == 0 else q_out.at[spot],
            q_out.at[spot],
            line_sem.at[step, (way + 1) // 2],
            chip_sem.at[origin],
            (row, (chip + way) * CORES + core),
        )
        onward = (chip + way >= 0) & (chip + way < n_chip)
        return copy, onward, (origin >= 0) & (origin < n_chip), spot, origin

    for way in (1, -1):
        copy, onward, _, _, _ = hop(0, way)

        @pl.when(onward)
        def _():
            copy.start()

    n_send = [
        remote(n_in, n_buf.at[k], send_sem.at[k], recv_sem.at[k], where)
        for k, where in enumerate(rows, 1)
    ]
    for copy in n_send:
        copy.start()
    e_send = [
        remote(
            e_in.at[where[0]], e_out.at[row], send_sem.at[n_row + k], recv_sem.at[n_row + k], where
        )
        for k, where in enumerate(rows, 1)
    ]
    for copy in e_send:
        copy.start()
    pair_send = remote(q_in, q_out.at[col], send_sem.at[0], recv_sem.at[0], sibling)
    pair_send.start()
    own = [
        pltpu.make_async_copy(q_in, q_out.at[col], own_sem.at[0]),
        pltpu.make_async_copy(e_in.at[row], e_out.at[row], own_sem.at[1]),
    ]
    weights = pltpu.make_async_copy(w_in, w_buf, own_sem.at[2])
    weights.start()
    for copy in own:
        copy.start()

    def project(rows_ref, spot):
        chunk = 2 * LANES
        hidden = rows_ref[...]

        @pl.loop(0, width // chunk)
        def _(step):
            left = pl.multiple_of(step * chunk, chunk)
            k_out[spot, :, pl.ds(left, chunk)] = jnp.dot(
                hidden, w_buf[:, pl.ds(left, chunk)], preferred_element_type=jnp.float32
            ).astype(k_out.dtype)
            right = pl.multiple_of(width + left, chunk)
            value = jnp.dot(hidden, w_buf[:, pl.ds(right, chunk)], preferred_element_type=jnp.float32)
            v_out[spot, pl.ds(left, chunk), :] = value.T.astype(v_out.dtype)

    weights.wait()
    project(n_in, row)

    def pass_on(step):
        for way in (1, -1):
            copy, onward, real, spot, origin = hop(step, way)

            @pl.when(real)
            def _():
                arrived = q_out.at[spot]
                copy.wait_recv()
                remote(
                    arrived,
                    arrived,
                    send_sem.at[2 * n_row + origin],
                    recv_sem.at[2 * n_row + origin],
                    sibling,
                ).start()

            if step < n_chip - 1:

                @pl.when(real & onward)
                def _():
                    hop(step, way)[0].start()

    for k in range(1, max(n_row, n_chip)):
        if k < n_chip:
            pass_on(k)
        if k < n_row:
            n_send[k - 1].wait_recv()
            project(n_buf.at[k], (row + n_row - k) % n_row)

    for way in (1, -1):
        for step in range(n_chip - 1):
            copy, onward, real, _, _ = hop(step, way)

            @pl.when(real & onward)
            def _():
                copy.wait_send()

        for step in range(1, n_chip):
            _, _, real, spot, origin = hop(step, way)

            @pl.when(real)
            def _():
                remote(
                    q_out.at[spot],
                    q_out.at[spot],
                    send_sem.at[2 * n_row + origin],
                    recv_sem.at[2 * n_row + origin],
                    sibling,
                ).wait()

    for copy in n_send:
        copy.wait_send()
    for copy in e_send + [pair_send]:
        copy.wait()
    for copy in own:
        copy.wait()


def attend(
    slot_cap, scale, pairs, slope, bias_ref, q_ref, k_ref, v_ref, e_ref, b_ref, o_ref, l_ref,
    m_acc, s_acc, o_acc, table, scores,
):
    query_count, heads, tile = l_ref.shape
    dim = q_ref.shape[2] // heads
    buckets_in = bias_ref.shape[0]
    m_acc[...] = jnp.full(m_acc.shape, LOW_FLOOR, jnp.float32)
    s_acc[...] = jnp.zeros(s_acc.shape, jnp.float32)
    o_acc[...] = jnp.zeros(o_acc.shape, jnp.float32)
    scores[0] = jnp.zeros(scores.shape[1:], jnp.float32)
    scores[0, :buckets_in, :heads] = bias_ref[...]
    table[...] = scores[0].T[:heads]

    def slot_step(slot, carry):
        query = pairs[0, slot]

        @pl.when(query >= 0)
        def _():
            key = pairs[1, slot] + slot // slot_cap
            buckets = b_ref[slot].T
            edges = e_ref[slot].astype(jnp.float32).T
            tops = []
            for h in range(heads):
                cols = slice(h * dim, (h + 1) * dim)
                score = lax.dot_general(
                    k_ref[key, :, cols],
                    q_ref[query, :, cols],
                    (((1,), (1,)), ((), ())),
                    preferred_element_type=jnp.float32,
                )
                entries = jnp.broadcast_to(table[h : h + 1, :], (tile, tile))
                bias = jnp.take_along_axis(entries, buckets, axis=1, mode="promise_in_bounds")
                score = score * scale + bias + slope[h] * edges
                scores[h] = score
                tops.append(jnp.max(score, axis=0, keepdims=True))
            old_max = m_acc[query]
            new_max = jnp.maximum(old_max, jnp.concatenate(tops, axis=0))
            keep = jnp.exp(old_max - new_max)
            m_acc[query] = new_max
            sums = []
            for h in range(heads):
                probs = jnp.exp(scores[h] - new_max[h : h + 1]).astype(jnp.bfloat16)
                sums.append(jnp.sum(probs.astype(jnp.float32), axis=0, keepdims=True))
                scores[h] = jnp.dot(
                    v_ref[key, h * dim : (h + 1) * dim, :], probs, preferred_element_type=jnp.float32
                )
            s_acc[query] = s_acc[query] * keep + jnp.concatenate(sums, axis=0)
            for h in range(heads):
                o_acc[query, h] = o_acc[query, h] * keep[h : h + 1] + scores[h]

        return carry

    lax.fori_loop(0, pairs.shape[1], slot_step, 0)

    def finish(query, carry):
        total = s_acc[query]
        live = total > 0.0
        safe = jnp.where(live, total, 1.0)
        l_ref[query] = jnp.where(live, m_acc[query] + jnp.log(safe), LOW_FLOOR)
        share = 1.0 / safe
        for h in range(heads):
            o_ref[query, h * dim : (h + 1) * dim, :] = (o_acc[query, h] * share[h : h + 1]).astype(
                o_ref.dtype
            )
        return carry

    lax.fori_loop(0, query_count, finish, 0)


def blend(levels, parts, heads):
    top = functools.reduce(jnp.maximum, levels)
    shares = [jnp.exp(level - top) for level in levels]
    total = functools.reduce(jnp.add, shares)
    weights = [share / total for share in shares]
    dim = parts[0].shape[0] // heads
    out = []
    for h in range(heads):
        rows = slice(h * dim, (h + 1) * dim)
        terms = [w[h : h + 1] * part[rows].astype(jnp.float32) for w, part in zip(weights, parts)]
        out.append(functools.reduce(jnp.add, terms))
    return out, top + jnp.log(total)


def combine(
    n_chip, o_ref, l_ref, a_ref, sib_o, sib_l, mix_o, mix_l, got_o, got_l, send_sem, recv_sem
):
    row, col = lax.axis_index("row"), lax.axis_index("col")
    chip, core = col // CORES, col % CORES
    heads = l_ref.shape[1]
    dim = o_ref.shape[1] // heads
    sibling = (row, chip * CORES + (1 - core))
    chips = [(row, ((chip + k) % n_chip) * CORES + core) for k in range(1, n_chip)]
    greet(chips + [sibling])

    def send(spot, src, dst, where):
        copy = pltpu.make_async_remote_copy(
            src_ref=src,
            dst_ref=dst,
            send_sem=send_sem.at[spot],
            recv_sem=recv_sem.at[spot],
            device_id=where,
            device_id_type=MESH,
        )
        copy.start()
        return copy

    order = list(range(1, n_chip)) + [0]
    to_sibling = {}
    for k in order:
        theirs = ((chip + k) % n_chip) * CORES + (1 - core)
        to_sibling[k] = [
            send(4 * k, l_ref.at[theirs], sib_l.at[k], sibling),
            send(4 * k + 1, o_ref.at[theirs], sib_o.at[k], sibling),
        ]
    over = []

    def push(k):
        over.append(send(4 * k + 2, mix_l.at[k], got_l.at[k], chips[k - 1]))
        over.append(send(4 * k + 3, mix_o.at[k], got_o.at[k], chips[k - 1]))

    for k in range(1, n_chip):
        for copy in to_sibling[k]:
            copy.wait_recv()
        mine = ((chip + k) % n_chip) * CORES + core
        out, level = blend([l_ref[mine], sib_l[k]], [o_ref[mine], sib_o[k]], heads)
        for h in range(heads):
            mix_o[k, h * dim : (h + 1) * dim, :] = out[h].astype(mix_o.dtype)
        mix_l[k] = level
        push(k)
    for copy in to_sibling[0]:
        copy.wait_recv()
    for copy in over:
        copy.wait_recv()
    levels = [l_ref[col], sib_l[0]] + [got_l[k] for k in range(1, n_chip)]
    parts = [o_ref[col], sib_o[0]] + [got_o[k] for k in range(1, n_chip)]
    out, _ = blend(levels, parts, heads)
    for h in range(heads):
        a_ref[h * dim : (h + 1) * dim, :] = out[h].astype(a_ref.dtype)
    for copies in to_sibling.values():
        for copy in copies:
            copy.wait_send()
    for copy in over:
        copy.wait_send()


def local(
    n_row,
    n_col,
    node_features,
    norm_gain,
    w_query,
    w_keyvalue,
    w_out,
    bias_table,
    edge_slope,
    pair_blocks,
    bucket_ids,
    edge_weight,
):
    tile, width = node_features.shape
    heads = edge_slope.shape[0]
    dim = width // heads
    n_chip = n_col // CORES
    slot_cap = edge_weight.shape[3]
    slots = n_row * slot_cap
    bf16, f32 = jnp.bfloat16, jnp.float32
    vmem = pl.BlockSpec(memory_space=pltpu.VMEM)
    smem = pl.BlockSpec(memory_space=pltpu.SMEM)
    hbm = pl.BlockSpec(memory_space=pl.ANY)

    normalized = normalize(node_features, norm_gain)
    queries = jnp.dot(normalized, w_query, preferred_element_type=f32).astype(bf16)
    copies = 2 * n_row + n_chip
    query_range, keys, values, edge_values = pl.pallas_call(
        functools.partial(exchange, n_row, n_chip),
        out_shape=(
            jax.ShapeDtypeStruct((n_col, tile, width), bf16),
            jax.ShapeDtypeStruct((n_row, tile, width), bf16),
            jax.ShapeDtypeStruct((n_row, width, tile), bf16),
            jax.ShapeDtypeStruct((n_row,) + edge_weight.shape[3:], edge_weight.dtype),
        ),
        in_specs=[vmem] * 3 + [hbm],
        out_specs=(hbm, vmem, vmem, hbm),
        scratch_shapes=[
            pltpu.VMEM((n_row, tile, width), bf16),
            pltpu.VMEM(w_keyvalue.shape, bf16),
            pltpu.SemaphoreType.DMA((copies,)),
            pltpu.SemaphoreType.DMA((copies,)),
            pltpu.SemaphoreType.DMA((n_chip,)),
            pltpu.SemaphoreType.DMA((n_chip, 2)),
            pltpu.SemaphoreType.DMA((3,)),
        ],
        compiler_params=pltpu.CompilerParams(
            collective_id=0, has_side_effects=True, vmem_limit_bytes=VMEM_LIMIT
        ),
        name="exchange",
    )(queries, normalized, edge_weight[0, 0], w_keyvalue)
    partial_out, partial_level = pl.pallas_call(
        functools.partial(attend, slot_cap, dim ** (-0.5)),
        out_shape=(
            jax.ShapeDtypeStruct((n_col, width, tile), bf16),
            jax.ShapeDtypeStruct((n_col, heads, tile), f32),
        ),
        in_specs=[smem, smem] + [vmem] * 6,
        out_specs=(vmem, vmem),
        scratch_shapes=[
            pltpu.VMEM((n_col, heads, tile), f32),
            pltpu.VMEM((n_col, heads, tile), f32),
            pltpu.VMEM((n_col, heads, dim, tile), f32),
            pltpu.VMEM((heads, tile), f32),
            pltpu.VMEM((heads, tile, tile), f32),
        ],
        compiler_params=pltpu.CompilerParams(vmem_limit_bytes=VMEM_LIMIT),
        name="attend",
    )(
        pair_blocks.reshape(2, slots),
        edge_slope,
        bias_table,
        query_range,
        keys,
        values,
        edge_values.reshape(slots, tile, tile),
        bucket_ids.reshape(slots, tile, tile),
    )
    attention = pl.pallas_call(
        functools.partial(combine, n_chip),
        out_shape=jax.ShapeDtypeStruct((width, tile), bf16),
        in_specs=[vmem] * 2,
        out_specs=vmem,
        scratch_shapes=[
            pltpu.VMEM((n_chip, width, tile), bf16),
            pltpu.VMEM((n_chip, heads, tile), f32),
        ]
        * 3
        + [pltpu.SemaphoreType.DMA((4 * n_chip,))] * 2,
        compiler_params=pltpu.CompilerParams(
            collective_id=1, has_side_effects=True, vmem_limit_bytes=VMEM_LIMIT
        ),
        name="combine",
    )(partial_out, partial_level)
    update = lax.dot_general(
        attention, w_out, (((0,), (0,)), ((), ())), preferred_element_type=f32
    )
    return (node_features.astype(f32) + update).astype(bf16)


def solution(mesh):
    return jax.shard_map(
        functools.partial(local, mesh.shape["row"], mesh.shape["col"]),
        mesh=mesh,
        in_specs=(
            P(("row", "col"), None),
            P(),
            P(),
            P(),
            P(),
            P(),
            P(),
            P("row", "col", None, None),
            P("row", "col", None, None, None),
            P("row", "col", None, None, None, None),
        ),
        out_specs=P(("row", "col"), None),
        check_vma=False,
    )
```

time: 115 us -> 83.1 us (0.72); the launches traced: 115 us -> 81.7 us
  Pallas kernels: 100 us -> 72.7 us
  matrix products: 10.1 us -> 4.02 us
    pallas_call x1, Pallas kernels: 29.7 us -> 14.4 us  [local(): pl.pallas_call(functools.partial(attend, slot_cap, dim ** (-0.5)), out_sh...]
    pallas_call x1, Pallas kernels: 29.7 us -> 22.5 us  [local(): pl.pallas_call(functools.partial(exchange, n_row, n_chip), out_shape=(jax...]
    dot_general x2 -> x1, matrix products: 8.99 us -> 2.87 us  [local(): lax.dot_general(attention, w_out, (((0,), (0,)), ((), ())), preferred_ele...]
    pallas_call x1, Pallas kernels: 40.9 us -> 35.8 us  [local(): pl.pallas_call(functools.partial(combine, n_chip), out_shape=jax.ShapeDty...]
    unnamed x6 -> x7, local copies, waits for them, and re-layouts: 0.01 us -> 1.38 us
    pad x1 -> x0, local copies, waits for them, and re-layouts: 1.29 us -> none  [local(): table = jnp.pad(bias_table.T, ((0, 0), (0, tile - bias_table.shape[0])))]
where the time goes in v2:
time: 83.1 us; the launch traced here: 81.7 us
  Pallas kernels  72.7 us (87%)
  matrix products  4.02 us (5%)
  other arithmetic  3.57 us (4%)
  local copies, waits for them, and re-layouts  1.38 us (2%)
    pallas_call x1, Pallas kernels, local(): pl.pallas_call(functools.partial(combine, n_chip), out_shape=jax.ShapeDty...  35.8 us
    pallas_call x1, Pallas kernels, local(): pl.pallas_call(functools.partial(exchange, n_row, n_chip), out_shape=(jax...  22.5 us
    pallas_call x1, Pallas kernels, local(): pl.pallas_call(functools.partial(attend, slot_cap, dim ** (-0.5)), out_sh...  14.4 us
    dot_general x1, matrix products, local(): lax.dot_general(attention, w_out, (((0,), (0,)), ((), ())), preferred_ele...  2.87 us

profile of v2, /device:TPU:15, one launch (start us, length us, event | category | flops | bytes accessed | tf_op | source)
XLA Modules:
  0.0 81.7 jit_solution(8038039504307324320)
XLA Ops:
  0.0 0.0 copy-start
  0.0 1.2 %convert_reduce_fusion = f32[128]{0:T(128)S(1)} fusion(bf16[128,1024]{1,0:T(8,128)(2,1)} %param.10), kind=kLoop, calls=%fused_computation.4 | loop fusion | flops 262016 | bytes 262656 | tf_op jit(solution)/shard_map/reduce_sum | solution.py:20
  1.2 1.2 %fusion.3 = f32[128]{0:T(128)S(1)} fusion(bf16[128,1024]{1,0:T(8,128)(2,1)} %param.10, f32[128]{0:T(128)S(1)} %broadcast_multiply_fusion), kind=kLoop, calls=%fused_computation.7 | loop fusion | flops 524160 | bytes 263168 | tf_op jit(solution)/shard_map/reduce_sum | solution.py:21
  2.4 1.4 %copy.11.bias_ref = f32[32,8]{1,0:T(8,128)} copy(f32[32,8]{0,1:T(8,128)} %param.15) | data formatting | bytes 2048 | tf_op args[5]
  3.8 1.2 %fusion.5.n_in = bf16[128,1024]{1,0:T(8,128)(2,1)S(1)} fusion(bf16[128,1024]{1,0:T(8,128)(2,1)} %param.10, f32[1024]{0:T(1024)} %param.11, f32[128]{0:T(128)S(1)} %add_rsqrt_fusion, f32[128]{0:T(128)S(1)} %broadcast_multiply_fusion), kind=kLoop, calls=%fused_computation.9 | loop fusion | flops 655360 | bytes 529408 | tf_op jit(solution)/shard_map/convert_element_type | solution.py:22
  4.9 0.0 copy-done
  5.0 0.0 copy-start.2
  5.0 1.2 %convolution_convert_fusion.q_in = bf16[128,1024]{1,0:T(8,128)(2,1)} fusion(bf16[128,1024]{1,0:T(8,128)(2,1)S(1)} %fusion.5.n_in, bf16[1024,1024]{1,0:T(8,128)(2,1)S(1)} %copy-done), kind=kOutput, calls=%fused_computation.1 | convolution fusion | flops 268566528 | bytes 2621440 | tf_op jit(solution)/shard_map/dot_general | solution.py:346
  6.1 0.0 copy-done.2
  6.1 22.5 %exchange.1 = (bf16[8,128,1024]{2,1,0:T(8,128)(2,1)}, bf16[4,128,1024]{2,1,0:T(8,128)(2,1)}, bf16[4,1024,128]{2,1,0:T(8,128)(2,1)}, bf16[4,4,128,128]{3,2,1,0:T(8,128)(2,1)}) custom-call(bf16[128,1024]{1,0:T(8,128)(2,1)} %convolution_convert_fusion.q_in, bf16[128,1024]{1,0:T(8,128)(2,1)} %copy-done.2, bf16[4,4,128,128]{3,2,1,0:T(8,128)(2,1)} %bitcast.9, ...), custom_call_target="tpu_custom_call" | custom-call | tf_op jit(solution)/shard_map/exchange/pallas_call | solution.py:348
  28.6 14.4 %attend.1 = (bf16[8,1024,128]{2,1,0:T(8,128)(2,1)}, f32[8,8,128]{2,1,0:T(8,128)}) custom-call(s32[2,16]{1,0:T(2,128)} %bitcast.11, f32[8]{0:T(128)} %slope.1, f32[32,8]{1,0:T(8,128)} %copy.11.bias_ref, bf16[8,128,1024]{2,1,0:T(8,128)(2,1)} %get-tuple-element.11.q_ref, bf16[4,128,1024]{2,1,0:T(8,128)(2,1)} %get-tuple-element.12.k_ref, ...), custom_call_target="tpu_custom_call" | custom-call | tf_op jit(solution)/shard_map/attend/pallas_call | solution.py:372
  43.0 0.0 copy-start.1
  43.0 35.8 %combine.1 = bf16[1024,128]{1,0:T(8,128)(2,1)} custom-call(bf16[8,1024,128]{2,1,0:T(8,128)(2,1)} %get-tuple-element.15.o_ref, f32[8,8,128]{2,1,0:T(8,128)} %get-tuple-element.16.l_ref), custom_call_target="tpu_custom_call" | custom-call | tf_op jit(solution)/shard_map/combine/pallas_call | solution.py:399
  78.8 0.0 copy-done.1
  78.8 2.9 %fusion = bf16[128,1024]{1,0:T(8,128)(2,1)} fusion(bf16[1024,128]{1,0:T(8,128)(2,1)} %combine.1, bf16[1024,1024]{1,0:T(8,128)(2,1)} %param.14, bf16[128,1024]{1,0:T(8,128)(2,1)S(1)} %copy-done.1), kind=kOutput, calls=%fused_computation.2 | convolution fusion | flops 268828672 | bytes 2883584 | tf_op jit(solution)/shard_map/dot_general | solution.py:415
  (2 shorter events, 0.0 us)
Async XLA Ops:
  0.0 5.0 %copy-start = (bf16[1024,1024]{1,0:T(8,128)(2,1)S(1)}, bf16[1024,1024]{1,0:T(8,128)(2,1)}, u32[]{:S(2)}) copy-start(bf16[1024,1024]{1,0:T(8,128)(2,1)} %param.12) | copy-start | bytes 6291460
  5.0 1.2 %copy-start.2 = (bf16[128,1024]{1,0:T(8,128)(2,1)}, bf16[128,1024]{1,0:T(8,128)(2,1)S(1)}, u32[]{:S(2)}) copy-start(bf16[128,1024]{1,0:T(8,128)(2,1)S(1)} %fusion.5.n_in) | copy-start | bytes 786436
  43.0 35.8 %copy-start.1 = (bf16[128,1024]{1,0:T(8,128)(2,1)S(1)}, bf16[128,1024]{1,0:T(8,128)(2,1)}, u32[]{:S(2)}) copy-start(bf16[128,1024]{1,0:T(8,128)(2,1)} %param.10) | copy-start | bytes 786436

commit v3 on v2

--- a/solution.py
+++ b/solution.py
@@ -30,8 +30,8 @@
 
 
 def exchange(
-    n_row, n_chip, q_in, n_in, e_in, w_in, q_out, k_out, v_out, e_out,
-    n_buf, w_buf, send_sem, recv_sem, chip_sem, line_sem, own_sem,
+    n_row, n_chip, x_in, gain_in, e_in, wq_in, w_in, q_out, k_out, v_out, e_out,
+    q_in, n_in, n_buf, wq_buf, w_buf, send_sem, recv_sem, chip_sem, line_sem, own_sem,
 ):
     row, col = lax.axis_index("row"), lax.axis_index("col")
     chip, core = col // CORES, col % CORES
@@ -39,6 +39,9 @@
     chips = [(row, ((chip + k) % n_chip) * CORES + core) for k in range(1, n_chip)]
     rows = [((row + k) % n_row, col) for k in range(1, n_row)]
     width = n_in.shape[1]
+    query_weights = pltpu.make_async_copy(wq_in, wq_buf, own_sem.at[3])
+    weights = pltpu.make_async_copy(w_in, w_buf, own_sem.at[2])
+    query_weights.start()
     greet(chips + [sibling] + rows)
 
     def remote(src, dst, send, recv, where):
@@ -64,25 +67,37 @@
         onward = (chip + way >= 0) & (chip + way < n_chip)
         return copy, onward, (origin >= 0) & (origin < n_chip), spot, origin
 
-    for way in (1, -1):
-        copy, onward, _, _, _ = hop(0, way)
-
-        @pl.when(onward)
-        def _():
-            copy.start()
-
-    n_send = [
-        remote(n_in, n_buf.at[k], send_sem.at[k], recv_sem.at[k], where)
-        for k, where in enumerate(rows, 1)
-    ]
-    for copy in n_send:
-        copy.start()
+    weights.start()
     e_send = [
         remote(
             e_in.at[where[0]], e_out.at[row], send_sem.at[n_row + k], recv_sem.at[n_row + k], where
         )
         for k, where in enumerate(rows, 1)
     ]
+    n_in[...] = normalize(x_in[...], gain_in[...])
+    query_weights.wait()
+    n_send = [
+        remote(n_in, n_buf.at[k], send_sem.at[k], recv_sem.at[k], where)
+        for k, where in enumerate(rows, 1)
+    ]
+    chunk = 2 * LANES
+
+    @pl.loop(0, width // chunk)
+    def _(step):
+        left = pl.multiple_of(step * chunk, chunk)
+        q_in[:, pl.ds(left, chunk)] = jnp.dot(
+            n_in[...], wq_buf[:, pl.ds(left, chunk)], preferred_element_type=jnp.float32
+        ).astype(q_in.dtype)
+
+    for copy in n_send:
+        copy.start()
+    for way in (1, -1):
+        copy, onward, _, _, _ = hop(0, way)
+
+        @pl.when(onward)
+        def _():
+            copy.start()
+
     for copy in e_send:
         copy.start()
     pair_send = remote(q_in, q_out.at[col], send_sem.at[0], recv_sem.at[0], sibling)
@@ -91,13 +106,10 @@
         pltpu.make_async_copy(q_in, q_out.at[col], own_sem.at[0]),
         pltpu.make_async_copy(e_in.at[row], e_out.at[row], own_sem.at[1]),
     ]
-    weights = pltpu.make_async_copy(w_in, w_buf, own_sem.at[2])
-    weights.start()
     for copy in own:
         copy.start()
 
     def project(rows_ref, spot):
-        chunk = 2 * LANES
         hidden = rows_ref[...]
 
         @pl.loop(0, width // chunk)
@@ -177,13 +189,12 @@
 ):
     query_count, heads, tile = l_ref.shape
     dim = q_ref.shape[2] // heads
-    buckets_in = bias_ref.shape[0]
+    buckets_in = bias_ref.shape[1]
     m_acc[...] = jnp.full(m_acc.shape, LOW_FLOOR, jnp.float32)
     s_acc[...] = jnp.zeros(s_acc.shape, jnp.float32)
     o_acc[...] = jnp.zeros(o_acc.shape, jnp.float32)
-    scores[0] = jnp.zeros(scores.shape[1:], jnp.float32)
-    scores[0, :buckets_in, :heads] = bias_ref[...]
-    table[...] = scores[0].T[:heads]
+    table[...] = jnp.zeros(table.shape, jnp.float32)
+    table[:, :buckets_in] = bias_ref[...]
 
     def slot_step(slot, carry):
         query = pairs[0, slot]
@@ -255,6 +266,13 @@
     return out, top + jnp.log(total)
 
 
+def partner(chip, k, n_chip):
+    if n_chip & (n_chip - 1):
+        return (chip + k) % n_chip
+    bits = [1 << b for b in range(n_chip.bit_length() - 1)]
+    return sum(((chip // bit + k // bit) % 2) * bit for bit in bits)
+
+
 def combine(
     n_chip, o_ref, l_ref, a_ref, sib_o, sib_l, mix_o, mix_l, got_o, got_l, send_sem, recv_sem
 ):
@@ -263,7 +281,7 @@
     heads = l_ref.shape[1]
     dim = o_ref.shape[1] // heads
     sibling = (row, chip * CORES + (1 - core))
-    chips = [(row, ((chip + k) % n_chip) * CORES + core) for k in range(1, n_chip)]
+    chips = [(row, partner(chip, k, n_chip) * CORES + core) for k in range(1, n_chip)]
     greet(chips + [sibling])
 
     def send(spot, src, dst, where):
@@ -278,10 +296,12 @@
         copy.start()
         return copy
 
-    order = list(range(1, n_chip)) + [0]
+    half = n_chip // 2
+    far = list(range(half, n_chip)) + list(range(1, half))
+    order = far + [0]
     to_sibling = {}
     for k in order:
-        theirs = ((chip + k) % n_chip) * CORES + (1 - core)
+        theirs = partner(chip, k, n_chip) * CORES + (1 - core)
         to_sibling[k] = [
             send(4 * k, l_ref.at[theirs], sib_l.at[k], sibling),
             send(4 * k + 1, o_ref.at[theirs], sib_o.at[k], sibling),
@@ -292,10 +312,10 @@
         over.append(send(4 * k + 2, mix_l.at[k], got_l.at[k], chips[k - 1]))
         over.append(send(4 * k + 3, mix_o.at[k], got_o.at[k], chips[k - 1]))
 
-    for k in range(1, n_chip):
+    for k in far:
         for copy in to_sibling[k]:
             copy.wait_recv()
-        mine = ((chip + k) % n_chip) * CORES + core
+        mine = partner(chip, k, n_chip) * CORES + core
         out, level = blend([l_ref[mine], sib_l[k]], [o_ref[mine], sib_o[k]], heads)
         for h in range(heads):
             mix_o[k, h * dim : (h + 1) * dim, :] = out[h].astype(mix_o.dtype)
@@ -342,8 +362,6 @@
     smem = pl.BlockSpec(memory_space=pltpu.SMEM)
     hbm = pl.BlockSpec(memory_space=pl.ANY)
 
-    normalized = normalize(node_features, norm_gain)
-    queries = jnp.dot(normalized, w_query, preferred_element_type=f32).astype(bf16)
     copies = 2 * n_row + n_chip
     query_range, keys, values, edge_values = pl.pallas_call(
         functools.partial(exchange, n_row, n_chip),
@@ -353,22 +371,25 @@
             jax.ShapeDtypeStruct((n_row, width, tile), bf16),
             jax.ShapeDtypeStruct((n_row,) + edge_weight.shape[3:], edge_weight.dtype),
         ),
-        in_specs=[vmem] * 3 + [hbm],
+        in_specs=[vmem] * 3 + [hbm] * 2,
         out_specs=(hbm, vmem, vmem, hbm),
         scratch_shapes=[
+            pltpu.VMEM((tile, width), bf16),
+            pltpu.VMEM((tile, width), bf16),
             pltpu.VMEM((n_row, tile, width), bf16),
+            pltpu.VMEM(w_query.shape, bf16),
             pltpu.VMEM(w_keyvalue.shape, bf16),
             pltpu.SemaphoreType.DMA((copies,)),
             pltpu.SemaphoreType.DMA((copies,)),
             pltpu.SemaphoreType.DMA((n_chip,)),
             pltpu.SemaphoreType.DMA((n_chip, 2)),
-            pltpu.SemaphoreType.DMA((3,)),
+            pltpu.SemaphoreType.DMA((4,)),
         ],
         compiler_params=pltpu.CompilerParams(
             collective_id=0, has_side_effects=True, vmem_limit_bytes=VMEM_LIMIT
         ),
         name="exchange",
-    )(queries, normalized, edge_weight[0, 0], w_keyvalue)
+    )(node_features, norm_gain[None], edge_weight[0, 0], w_query, w_keyvalue)
     partial_out, partial_level = pl.pallas_call(
         functools.partial(attend, slot_cap, dim ** (-0.5)),
         out_shape=(
@@ -389,7 +410,7 @@
     )(
         pair_blocks.reshape(2, slots),
         edge_slope,
-        bias_table,
+        bias_table.T,
         query_range,
         keys,
         values,

time: 83.1 us -> 77.7 us (0.935); the launches traced: 81.7 us -> 77.3 us
  other arithmetic: 3.57 us -> 0 us
  Pallas kernels: 72.7 us -> 75.1 us
  matrix products: 4.02 us -> 2.13 us
  local copies, waits for them, and re-layouts: 1.38 us -> 0.01 us
    pallas_call x1, Pallas kernels: 35.8 us -> 39.5 us  [local(): pl.pallas_call(functools.partial(combine, n_chip), out_shape=jax.ShapeDty...]
    pallas_call x1, Pallas kernels: 14.4 us -> 11.2 us  [local(): pl.pallas_call(functools.partial(attend, slot_cap, dim ** (-0.5)), out_sh...]
    reduce_sum x2 -> x0, other arithmetic: 2.38 us -> none  [the longest x1 1.21 us: normalize(): centered = as_float - jnp.mean(as_float, axis=-1, keepdims=True)]
    pallas_call x1, Pallas kernels: 22.5 us -> 24.5 us  [local(): pl.pallas_call(functools.partial(exchange, n_row, n_chip), out_shape=(jax...]
    unnamed x7 -> x4, local copies, waits for them, and re-layouts: 1.38 us -> 0.01 us
    convert_element_type x1 -> x0, other arithmetic: 1.17 us -> none  [normalize(): (centered * lax.rsqrt(variance + EPSILON) * gain_vec).astype(jnp.bfloat16)]
    dot_general x1 -> x0, matrix products: 1.15 us -> none  [local(): jnp.dot(normalized, w_query, preferred_element_type=f32).astype(bf16)]
where the time goes in v3:
time: 77.7 us; the launch traced here: 77.3 us
  Pallas kernels  75.1 us (97%)
  matrix products  2.13 us (3%)
    pallas_call x1, Pallas kernels, local(): pl.pallas_call(functools.partial(combine, n_chip), out_shape=jax.ShapeDty...  39.5 us
    pallas_call x1, Pallas kernels, local(): pl.pallas_call(functools.partial(exchange, n_row, n_chip), out_shape=(jax...  24.5 us
    pallas_call x1, Pallas kernels, local(): pl.pallas_call(functools.partial(attend, slot_cap, dim ** (-0.5)), out_sh...  11.2 us
    dot_general x1, matrix products, local(): lax.dot_general(attention, w_out, (((0,), (0,)), ((), ())), preferred_ele...  2.13 us

profile of v3, /device:TPU:15, one launch (start us, length us, event | category | flops | bytes accessed | tf_op | source)
XLA Modules:
  0.0 77.3 jit_solution(14015779464297737395)
XLA Ops:
  0.0 0.0 copy-start
  0.0 24.5 %exchange.1 = (bf16[8,128,1024]{2,1,0:T(8,128)(2,1)}, bf16[4,128,1024]{2,1,0:T(8,128)(2,1)}, bf16[4,1024,128]{2,1,0:T(8,128)(2,1)}, bf16[4,4,128,128]{3,2,1,0:T(8,128)(2,1)}) custom-call(bf16[128,1024]{1,0:T(8,128)(2,1)} %x_in.1, f32[1,1024]{1,0:T(1,128)} %bitcast.11, bf16[4,4,128,128]{3,2,1,0:T(8,128)(2,1)} %bitcast.9, bf16[1024,1024]{1,0:T(8,128)(2,1)} %wq_in.1, ...), custom_call_target="tpu_custom_call" | custom-call | tf_op jit(solution)/shard_map/exchange/pallas_call | solution.py:366
  24.5 11.2 %attend.1 = (bf16[8,1024,128]{2,1,0:T(8,128)(2,1)}, f32[8,8,128]{2,1,0:T(8,128)}) custom-call(s32[2,16]{1,0:T(2,128)} %bitcast.13, f32[8]{0:T(128)} %slope.1, f32[8,32]{1,0:T(8,128)} %bitcast.12, bf16[8,128,1024]{2,1,0:T(8,128)(2,1)} %get-tuple-element.11.q_ref, bf16[4,128,1024]{2,1,0:T(8,128)(2,1)} %get-tuple-element.12.k_ref, ...), custom_call_target="tpu_custom_call" | custom-call | tf_op jit(solution)/shard_map/attend/pallas_call | solution.py:393
  35.7 0.0 copy-start.1
  35.7 39.5 %combine.1 = bf16[1024,128]{1,0:T(8,128)(2,1)} custom-call(bf16[8,1024,128]{2,1,0:T(8,128)(2,1)} %get-tuple-element.15.o_ref, f32[8,8,128]{2,1,0:T(8,128)} %get-tuple-element.16.l_ref), custom_call_target="tpu_custom_call" | custom-call | tf_op jit(solution)/shard_map/combine/pallas_call | solution.py:420
  75.1 0.0 copy-done
  75.2 0.0 copy-done.1
  75.2 2.1 %fusion = bf16[128,1024]{1,0:T(8,128)(2,1)} fusion(bf16[1024,128]{1,0:T(8,128)(2,1)} %combine.1, bf16[1024,1024]{1,0:T(8,128)(2,1)S(1)} %copy-done, bf16[128,1024]{1,0:T(8,128)(2,1)S(1)} %copy-done.1), kind=kOutput, calls=%fused_computation.1 | convolution fusion | flops 268828672 | bytes 2883584 | tf_op jit(solution)/shard_map/dot_general | solution.py:436
Async XLA Ops:
  0.0 75.1 %copy-start = (bf16[1024,1024]{1,0:T(8,128)(2,1)S(1)}, bf16[1024,1024]{1,0:T(8,128)(2,1)}, u32[]{:S(2)}) copy-start(bf16[1024,1024]{1,0:T(8,128)(2,1)} %param.14) | copy-start | bytes 6291460
  35.7 39.5 %copy-start.1 = (bf16[128,1024]{1,0:T(8,128)(2,1)S(1)}, bf16[128,1024]{1,0:T(8,128)(2,1)}, u32[]{:S(2)}) copy-start(bf16[128,1024]{1,0:T(8,128)(2,1)} %x_in.1) | copy-start | bytes 786436

commit v4 on v3

--- a/solution.py
+++ b/solution.py
@@ -184,9 +184,28 @@
 
 
 def attend(
-    slot_cap, scale, pairs, slope, bias_ref, q_ref, k_ref, v_ref, e_ref, b_ref, o_ref, l_ref,
-    m_acc, s_acc, o_acc, table, scores,
+    slot_cap, scale, pairs, slope, bias_ref, q_in, k_in, v_in, e_in, b_in, o_out, l_ref,
+    m_acc, s_acc, o_acc, table, scores, q_ref, k_ref, v_ref, e_ref, b_ref, o_ref,
+    whole_sem, slot_sem, out_sem,
 ):
+    whole = [
+        pltpu.make_async_copy(src, dst, whole_sem.at[i])
+        for i, (src, dst) in enumerate(((q_in, q_ref), (k_in, k_ref), (v_in, v_ref)))
+    ]
+    for copy in whole:
+        copy.start()
+
+    def fetch(slot):
+        return (
+            pltpu.make_async_copy(b_in.at[slot], b_ref.at[slot], slot_sem.at[0, slot]),
+            pltpu.make_async_copy(e_in.at[slot], e_ref.at[slot], slot_sem.at[1, slot]),
+        )
+
+    @pl.loop(0, pairs.shape[1])
+    def _(slot):
+        for copy in fetch(slot):
+            copy.start()
+
     query_count, heads, tile = l_ref.shape
     dim = q_ref.shape[2] // heads
     buckets_in = bias_ref.shape[1]
@@ -196,7 +215,12 @@
     table[...] = jnp.zeros(table.shape, jnp.float32)
     table[:, :buckets_in] = bias_ref[...]
 
+    for copy in whole:
+        copy.wait()
+
     def slot_step(slot, carry):
+        for copy in fetch(slot):
+            copy.wait()
         query = pairs[0, slot]
 
         @pl.when(query >= 0)
@@ -247,9 +271,17 @@
             o_ref[query, h * dim : (h + 1) * dim, :] = (o_acc[query, h] * share[h : h + 1]).astype(
                 o_ref.dtype
             )
+        give(query).start()
         return carry
 
+    def give(query):
+        return pltpu.make_async_copy(o_ref.at[query], o_out.at[query], out_sem.at[query])
+
     lax.fori_loop(0, query_count, finish, 0)
+
+    @pl.loop(0, query_count)
+    def _(query):
+        give(query).wait()
 
 
 def blend(levels, parts, heads):
@@ -274,7 +306,8 @@
 
 
 def combine(
-    n_chip, o_ref, l_ref, a_ref, sib_o, sib_l, mix_o, mix_l, got_o, got_l, send_sem, recv_sem
+    n_chip, o_ref, l_ref, a_ref, sib_o, sib_l, mix_o, mix_l, got_o, got_l, own_o,
+    send_sem, recv_sem, own_sem,
 ):
     row, col = lax.axis_index("row"), lax.axis_index("col")
     chip, core = col // CORES, col % CORES
@@ -282,6 +315,14 @@
     dim = o_ref.shape[1] // heads
     sibling = (row, chip * CORES + (1 - core))
     chips = [(row, partner(chip, k, n_chip) * CORES + core) for k in range(1, n_chip)]
+    own = [
+        pltpu.make_async_copy(
+            o_ref.at[partner(chip, k, n_chip) * CORES + core], own_o.at[k], own_sem.at[k]
+        )
+        for k in range(n_chip)
+    ]
+    for copy in own:
+        copy.start()
     greet(chips + [sibling])
 
     def send(spot, src, dst, where):
@@ -315,8 +356,9 @@
     for k in far:
         for copy in to_sibling[k]:
             copy.wait_recv()
+        own[k].wait()
         mine = partner(chip, k, n_chip) * CORES + core
-        out, level = blend([l_ref[mine], sib_l[k]], [o_ref[mine], sib_o[k]], heads)
+        out, level = blend([l_ref[mine], sib_l[k]], [own_o[k], sib_o[k]], heads)
         for h in range(heads):
             mix_o[k, h * dim : (h + 1) * dim, :] = out[h].astype(mix_o.dtype)
         mix_l[k] = level
@@ -325,8 +367,9 @@
         copy.wait_recv()
     for copy in over:
         copy.wait_recv()
+    own[0].wait()
     levels = [l_ref[col], sib_l[0]] + [got_l[k] for k in range(1, n_chip)]
-    parts = [o_ref[col], sib_o[0]] + [got_o[k] for k in range(1, n_chip)]
+    parts = [own_o[0], sib_o[0]] + [got_o[k] for k in range(1, n_chip)]
     out, _ = blend(levels, parts, heads)
     for h in range(heads):
         a_ref[h * dim : (h + 1) * dim, :] = out[h].astype(a_ref.dtype)
@@ -396,14 +439,23 @@
             jax.ShapeDtypeStruct((n_col, width, tile), bf16),
             jax.ShapeDtypeStruct((n_col, heads, tile), f32),
         ),
-        in_specs=[smem, smem] + [vmem] * 6,
-        out_specs=(vmem, vmem),
+        in_specs=[smem, smem, vmem] + [hbm] * 5,
+        out_specs=(hbm, vmem),
         scratch_shapes=[
             pltpu.VMEM((n_col, heads, tile), f32),
             pltpu.VMEM((n_col, heads, tile), f32),
             pltpu.VMEM((n_col, heads, dim, tile), f32),
             pltpu.VMEM((heads, tile), f32),
             pltpu.VMEM((heads, tile, tile), f32),
+            pltpu.VMEM(query_range.shape, bf16),
+            pltpu.VMEM(keys.shape, bf16),
+            pltpu.VMEM(values.shape, bf16),
+            pltpu.VMEM((slots, tile, tile), bf16),
+            pltpu.VMEM((slots, tile, tile), jnp.int32),
+            pltpu.VMEM((n_col, width, tile), bf16),
+            pltpu.SemaphoreType.DMA((3,)),
+            pltpu.SemaphoreType.DMA((2, slots)),
+            pltpu.SemaphoreType.DMA((n_col,)),
         ],
         compiler_params=pltpu.CompilerParams(vmem_limit_bytes=VMEM_LIMIT),
         name="attend",
@@ -420,14 +472,16 @@
     attention = pl.pallas_call(
         functools.partial(combine, n_chip),
         out_shape=jax.ShapeDtypeStruct((width, tile), bf16),
-        in_specs=[vmem] * 2,
+        in_specs=[hbm, vmem],
         out_specs=vmem,
         scratch_shapes=[
             pltpu.VMEM((n_chip, width, tile), bf16),
             pltpu.VMEM((n_chip, heads, tile), f32),
         ]
         * 3
-        + [pltpu.SemaphoreType.DMA((4 * n_chip,))] * 2,
+        + [pltpu.VMEM((n_chip, width, tile), bf16)]
+        + [pltpu.SemaphoreType.DMA((4 * n_chip,))] * 2
+        + [pltpu.SemaphoreType.DMA((n_chip,))],
         compiler_params=pltpu.CompilerParams(
             collective_id=1, has_side_effects=True, vmem_limit_bytes=VMEM_LIMIT
         ),

time: 77.7 us -> 75.7 us (0.974)
  Pallas kernels: 75.1 us -> 73.4 us
    pallas_call x1, Pallas kernels: 39.5 us -> 34.7 us  [local(): pl.pallas_call(functools.partial(combine, n_chip), out_shape=jax.ShapeDty...]
    pallas_call x1, Pallas kernels: 11.2 us -> 14.2 us  [local(): pl.pallas_call(functools.partial(attend, slot_cap, dim ** (-0.5)), out_sh...]
where the time goes in v4:
time: 75.7 us; the launch traced here: 75.6 us
  Pallas kernels  73.4 us (97%)
  matrix products  2.13 us (3%)
    pallas_call x1, Pallas kernels, local(): pl.pallas_call(functools.partial(combine, n_chip), out_shape=jax.ShapeDty...  34.7 us
    pallas_call x1, Pallas kernels, local(): pl.pallas_call(functools.partial(exchange, n_row, n_chip), out_shape=(jax...  24.5 us
    pallas_call x1, Pallas kernels, local(): pl.pallas_call(functools.partial(attend, slot_cap, dim ** (-0.5)), out_sh...  14.2 us
    dot_general x1, matrix products, local(): lax.dot_general(attention, w_out, (((0,), (0,)), ((), ())), preferred_ele...  2.13 us

profile of v4, /device:TPU:15, one launch (start us, length us, event | category | flops | bytes accessed | tf_op | source)
XLA Modules:
  0.0 75.6 jit_solution(663477261985423030)
XLA Ops:
  0.0 0.0 copy-start
  0.0 24.5 %exchange.1 = (bf16[8,128,1024]{2,1,0:T(8,128)(2,1)}, bf16[4,128,1024]{2,1,0:T(8,128)(2,1)}, bf16[4,1024,128]{2,1,0:T(8,128)(2,1)}, bf16[4,4,128,128]{3,2,1,0:T(8,128)(2,1)}) custom-call(bf16[128,1024]{1,0:T(8,128)(2,1)} %x_in.1, f32[1,1024]{1,0:T(1,128)} %bitcast.11, bf16[4,4,128,128]{3,2,1,0:T(8,128)(2,1)} %bitcast.9, bf16[1024,1024]{1,0:T(8,128)(2,1)} %wq_in.1, ...), custom_call_target="tpu_custom_call" | custom-call | tf_op jit(solution)/shard_map/exchange/pallas_call | solution.py:409
  24.5 14.2 %attend.1 = (bf16[8,1024,128]{2,1,0:T(8,128)(2,1)}, f32[8,8,128]{2,1,0:T(8,128)}) custom-call(s32[2,16]{1,0:T(2,128)} %bitcast.13, f32[8]{0:T(128)} %slope.1, f32[8,32]{1,0:T(8,128)} %bitcast.12, bf16[8,128,1024]{2,1,0:T(8,128)(2,1)} %get-tuple-element.11.q_in, bf16[4,128,1024]{2,1,0:T(8,128)(2,1)} %get-tuple-element.12.k_in, ...), custom_call_target="tpu_custom_call" | custom-call | tf_op jit(solution)/shard_map/attend/pallas_call | solution.py:436
  38.7 0.0 copy-start.1
  38.7 34.7 %combine.1 = bf16[1024,128]{1,0:T(8,128)(2,1)} custom-call(bf16[8,1024,128]{2,1,0:T(8,128)(2,1)} %get-tuple-element.15.o_ref, f32[8,8,128]{2,1,0:T(8,128)} %get-tuple-element.16.l_ref), custom_call_target="tpu_custom_call" | custom-call | tf_op jit(solution)/shard_map/combine/pallas_call | solution.py:472
  73.5 0.0 copy-done
  73.5 0.0 copy-done.1
  73.5 2.1 %fusion = bf16[128,1024]{1,0:T(8,128)(2,1)} fusion(bf16[1024,128]{1,0:T(8,128)(2,1)} %combine.1, bf16[1024,1024]{1,0:T(8,128)(2,1)S(1)} %copy-done, bf16[128,1024]{1,0:T(8,128)(2,1)S(1)} %copy-done.1), kind=kOutput, calls=%fused_computation.1 | convolution fusion | flops 268828672 | bytes 2883584 | tf_op jit(solution)/shard_map/dot_general | solution.py:490
Async XLA Ops:
  0.0 73.5 %copy-start = (bf16[1024,1024]{1,0:T(8,128)(2,1)S(1)}, bf16[1024,1024]{1,0:T(8,128)(2,1)}, u32[]{:S(2)}) copy-start(bf16[1024,1024]{1,0:T(8,128)(2,1)} %param.14) | copy-start | bytes 6291460
  38.7 34.8 %copy-start.1 = (bf16[128,1024]{1,0:T(8,128)(2,1)S(1)}, bf16[128,1024]{1,0:T(8,128)(2,1)}, u32[]{:S(2)}) copy-start(bf16[128,1024]{1,0:T(8,128)(2,1)} %x_in.1) | copy-start | bytes 786436

commit v5 on v3

--- a/solution.py
+++ b/solution.py
@@ -12,7 +12,7 @@
 CORES = 2
 MESH = pl.DeviceIdType.MESH
 LANES = 128
-VMEM_LIMIT = 60 * 2**20
+ROOM = 6 * 2**20
 
 
 def normalize(features, gain_vec):
@@ -362,6 +362,11 @@
     smem = pl.BlockSpec(memory_space=pltpu.SMEM)
     hbm = pl.BlockSpec(memory_space=pl.ANY)
 
+    block = 2 * tile * width
+    weight_bytes = 2 * (w_query.size + w_keyvalue.size)
+    exchange_bytes = (3 * n_row + 4) * block + weight_bytes + 2 * edge_weight.size
+    attend_bytes = (4 * n_col + 2 * n_row) * block + 6 * slots * tile * tile
+    combine_bytes = (n_col + 3 * n_chip + 2) * block
     copies = 2 * n_row + n_chip
     query_range, keys, values, edge_values = pl.pallas_call(
         functools.partial(exchange, n_row, n_chip),
@@ -386,7 +391,7 @@
             pltpu.SemaphoreType.DMA((4,)),
         ],
         compiler_params=pltpu.CompilerParams(
-            collective_id=0, has_side_effects=True, vmem_limit_bytes=VMEM_LIMIT
+            collective_id=0, has_side_effects=True, vmem_limit_bytes=exchange_bytes + ROOM
         ),
         name="exchange",
     )(node_features, norm_gain[None], edge_weight[0, 0], w_query, w_keyvalue)
@@ -405,7 +410,7 @@
             pltpu.VMEM((heads, tile), f32),
             pltpu.VMEM((heads, tile, tile), f32),
         ],
-        compiler_params=pltpu.CompilerParams(vmem_limit_bytes=VMEM_LIMIT),
+        compiler_params=pltpu.CompilerParams(vmem_limit_bytes=attend_bytes + ROOM),
         name="attend",
     )(
         pair_blocks.reshape(2, slots),
@@ -429,7 +434,7 @@
         * 3
         + [pltpu.SemaphoreType.DMA((4 * n_chip,))] * 2,
         compiler_params=pltpu.CompilerParams(
-            collective_id=1, has_side_effects=True, vmem_limit_bytes=VMEM_LIMIT
+            collective_id=1, has_side_effects=True, vmem_limit_bytes=combine_bytes + ROOM
         ),
         name="combine",
     )(partial_out, partial_level)

time: 77.7 us -> 74.2 us (0.955)
  the two profiles are of different devices: /device:TPU:15 before, /device:TPU:13 now
where the time goes in v5:
time: 74.2 us; the launch traced here: 73.1 us
  Pallas kernels  65.2 us (88%)
  local copies, waits for them, and re-layouts  6.63 us (9%)
  matrix products  1.18 us (2%)
    pallas_call x1, Pallas kernels, local(): pl.pallas_call(functools.partial(combine, n_chip), out_shape=jax.ShapeDty...  33.2 us
    pallas_call x1, Pallas kernels, local(): pl.pallas_call(functools.partial(exchange, n_row, n_chip), out_shape=(jax...  22.7 us
    pallas_call x1, Pallas kernels, local(): pl.pallas_call(functools.partial(attend, slot_cap, dim ** (-0.5)), out_sh...  9.3 us
    unnamed x22, local copies, waits for them, and re-layouts  6.63 us

profile of v5, /device:TPU:13, one launch (start us, length us, event | category | flops | bytes accessed | tf_op | source)
XLA Modules:
  0.0 73.1 jit_solution(9749129611511389745)
XLA Ops:
  0.0 0.0 copy-start
  0.0 0.0 copy-start.1
  0.0 2.3 %copy-done.1 = bf16[1024,2048]{1,0:T(8,128)(2,1)S(1)} copy-done((bf16[1024,2048]{1,0:T(8,128)(2,1)S(1)}, bf16[1024,2048]{1,0:T(8,128)(2,1)}, u32[]{:S(2)}) %copy-start.1) | copy-done | bytes 4194328
  2.3 0.0 copy-start.2
  2.3 1.6 %copy-done.2 = bf16[1024,1024]{1,0:T(8,128)(2,1)S(1)} copy-done((bf16[1024,1024]{1,0:T(8,128)(2,1)S(1)}, bf16[1024,1024]{1,0:T(8,128)(2,1)}, u32[]{:S(2)}) %copy-start.2) | copy-done | bytes 2097176
  3.9 0.0 copy-start.4
  3.9 0.9 %copy-done.4 = bf16[128,1024]{1,0:T(8,128)(2,1)S(1)} copy-done((bf16[128,1024]{1,0:T(8,128)(2,1)S(1)}, bf16[128,1024]{1,0:T(8,128)(2,1)}, u32[]{:S(2)}) %copy-start.4) | copy-done | bytes 262168
  4.9 0.0 copy-start.6
  4.9 1.0 %copy-done.6 = bf16[1,1,4,4,128,128]{5,4,3,2,1,0:T(8,128)(2,1)S(1)} copy-done((bf16[1,1,4,4,128,128]{5,4,3,2,1,0:T(8,128)(2,1)S(1)}, bf16[1,1,4,4,128,128]{5,4,3,2,1,0:T(8,128)(2,1)}, u32[]{:S(2)}) %copy-start.6) | copy-done | bytes 524312
  5.9 0.0 copy-start.7
  5.9 0.7 copy-done.7
  6.6 0.0 copy-start.3
  6.6 0.0 copy-start.8
  6.6 0.0 copy-start.9
  6.6 0.0 copy-start.10
  6.6 22.7 %exchange.1 = (bf16[8,128,1024]{2,1,0:T(8,128)(2,1)S(1)}, bf16[4,128,1024]{2,1,0:T(8,128)(2,1)S(1)}, bf16[4,1024,128]{2,1,0:T(8,128)(2,1)S(1)}, bf16[4,4,128,128]{3,2,1,0:T(8,128)(2,1)S(1)}) custom-call(bf16[128,1024]{1,0:T(8,128)(2,1)S(1)} %copy-done.4, f32[1,1024]{1,0:T(1,128)S(1)} %bitcast.11, bf16[4,4,128,128]{3,2,1,0:T(8,128)(2,1)S(1)} %bitcast.9, ...), custom_call_target="tpu_custom_call" | custom-call | tf_op jit(solution)/shard_map/exchange/pallas_call | solution.py:371
  29.3 0.0 copy-done.3
  29.3 0.0 copy-done.8
  29.3 0.0 copy-done.9
  29.3 0.0 copy-done.10
  29.4 9.3 %attend.1 = (bf16[8,1024,128]{2,1,0:T(8,128)(2,1)S(1)}, f32[8,8,128]{2,1,0:T(8,128)S(1)}) custom-call(s32[2,16]{1,0:T(2,128)S(1)} %bitcast.13, f32[8]{0:T(128)S(1)} %copy-done.10, f32[8,32]{1,0:T(8,128)S(1)} %bitcast.12, bf16[8,128,1024]{2,1,0:T(8,128)(2,1)S(1)} %get-tuple-element.11.q_ref, bf16[4,128,1024]{2,1,0:T(8,128)(2,1)S(1)} %get-tuple-element.12.k_ref, ...), custom_call_target="tpu_custom_call" | custom-call | tf_op jit(solution)/shard_map/attend/pallas_call | solution.py:398
  38.7 0.0 copy-start.5
  38.7 33.2 %combine.1 = bf16[1024,128]{1,0:T(8,128)(2,1)S(1)} custom-call(bf16[8,1024,128]{2,1,0:T(8,128)(2,1)S(1)} %get-tuple-element.15.o_ref, f32[8,8,128]{2,1,0:T(8,128)S(1)} %get-tuple-element.16.l_ref), custom_call_target="tpu_custom_call" | custom-call | tf_op jit(solution)/shard_map/combine/pallas_call | solution.py:425
  71.9 0.0 copy-done
  71.9 0.0 copy-done.5
  71.9 1.2 %fusion = bf16[128,1024]{1,0:T(8,128)(2,1)} fusion(bf16[1024,128]{1,0:T(8,128)(2,1)S(1)} %combine.1, bf16[1024,1024]{1,0:T(8,128)(2,1)S(1)} %copy-done, bf16[128,1024]{1,0:T(8,128)(2,1)S(1)} %copy-done.5), kind=kOutput, calls=%fused_computation.1 | convolution fusion | flops 268828672 | bytes 2883584 | tf_op jit(solution)/shard_map/dot_general | solution.py:441
Async XLA Ops:
  0.0 71.9 %copy-start = (bf16[1024,1024]{1,0:T(8,128)(2,1)S(1)}, bf16[1024,1024]{1,0:T(8,128)(2,1)}, u32[]{:S(2)}) copy-start(bf16[1024,1024]{1,0:T(8,128)(2,1)} %param.14) | copy-start | bytes 6291460
  0.0 2.3 %copy-start.1 = (bf16[1024,2048]{1,0:T(8,128)(2,1)S(1)}, bf16[1024,2048]{1,0:T(8,128)(2,1)}, u32[]{:S(2)}) copy-start(bf16[1024,2048]{1,0:T(8,128)(2,1)} %w_in.1) | copy-start | bytes 12582916
  2.3 1.6 %copy-start.2 = (bf16[1024,1024]{1,0:T(8,128)(2,1)S(1)}, bf16[1024,1024]{1,0:T(8,128)(2,1)}, u32[]{:S(2)}) copy-start(bf16[1024,1024]{1,0:T(8,128)(2,1)} %wq_in.1) | copy-start | bytes 6291460
  3.9 0.9 %copy-start.4 = (bf16[128,1024]{1,0:T(8,128)(2,1)S(1)}, bf16[128,1024]{1,0:T(8,128)(2,1)}, u32[]{:S(2)}) copy-start(bf16[128,1024]{1,0:T(8,128)(2,1)} %x_in.1) | copy-start | bytes 786436
  4.9 1.0 %copy-start.6 = (bf16[1,1,4,4,128,128]{5,4,3,2,1,0:T(8,128)(2,1)S(1)}, bf16[1,1,4,4,128,128]{5,4,3,2,1,0:T(8,128)(2,1)}, u32[]{:S(2)}) copy-start(bf16[1,1,4,4,128,128]{5,4,3,2,1,0:T(8,128)(2,1)} %param.19) | copy-start | bytes 1572868
  5.9 0.7 copy-start.7
  6.6 22.7 %copy-start.3 = (s32[1,1,16,128,128]{4,3,2,1,0:T(8,128)S(1)}, s32[1,1,16,128,128]{4,3,2,1,0:T(8,128)}, u32[]{:S(2)}) copy-start(s32[1,1,16,128,128]{4,3,2,1,0:T(8,128)} %param.18) | copy-start | bytes 3145732
  6.6 22.7 %copy-start.8 = (f32[32,8]{0,1:T(8,128)S(1)}, f32[32,8]{0,1:T(8,128)}, u32[]{:S(2)}) copy-start(f32[32,8]{0,1:T(8,128)} %param.15) | copy-start | bytes 3076
  6.6 22.7 %copy-start.9 = (s32[1,1,2,16]{3,2,1,0:T(2,128)S(1)}, s32[1,1,2,16]{3,2,1,0:T(2,128)}, u32[]{:S(2)}) copy-start(s32[1,1,2,16]{3,2,1,0:T(2,128)} %param.17) | copy-start | bytes 388
  6.6 22.7 %copy-start.10 = (f32[8]{0:T(128)S(1)}, f32[8]{0:T(128)}, u32[]{:S(2)}) copy-start(f32[8]{0:T(128)} %slope.1) | copy-start | bytes 100
  38.7 33.2 %copy-start.5 = (bf16[128,1024]{1,0:T(8,128)(2,1)S(1)}, bf16[128,1024]{1,0:T(8,128)(2,1)}, u32[]{:S(2)}) copy-start(bf16[128,1024]{1,0:T(8,128)(2,1)} %x_in.1) | copy-start | bytes 786436
